TPU v7x, 128 devices: a whole 4x4x4 slice. The times are simulated.
128 devices in a mesh: slab: 8 (over x, y_hi), tile: 16 (over y_lo, z, core).
Axes of the slice: x: 4, y: 4 (y_hi: 2, y_lo: 2; y = y_hi * 2 + y_lo), z: 4, core: 2. Of those that a mesh axis runs over, the one named last changes fastest.
Arguments:
- particles: float32 [7, 16, 32, 1536], P(None, 'slab', 'tile')
- counts: int32 [16, 32, 48], P('slab', 'tile'), may hold values from 10 to 32, as said below
- leavers: int32 [2, 8, 32, 48], P(None, 'slab', 'tile'), may hold values from 0 to 4, as said below
Outputs:
- kept: float32 [7, 16, 32, 1536], P(None, 'slab', 'tile')
- arrivals: float32 [2, 7, 24576], P(None, None, ('slab', 'tile'))
Inputs may be any that keep to these rules, and one draw needn't show every extreme that they name: `counts`: one cell holds exactly 32. Over the 2 x 48 cells of one face of one device the leavers sum to exactly 192; one face cell of each face has 4.
All inputs are finite; a program needn't handle non-finite values.
Results may differ from a plain program's by a relative error of at most 0.0003.
Values sent between devices are 32-bit elements; how exact they have to be, the bound alone decides.
No kernel may reach another device: no remote copies, remote signals or barrier semaphores. Data moves between devices by JAX's collectives and lax.ppermute only.
A program may use at most 128 MiB of HBM per device.

v0:
```python
import math

import jax
import jax.numpy as jnp
from jax import lax
from jax.sharding import PartitionSpec as P

SLOTS = 32
LMAX = 4


sound_speed = 10.0
smoothing = 0.5
cell_side = 2.0 * smoothing
kernel_norm = 21.0 / (16.0 * math.pi * smoothing**3)
grad_scale = -5.0 * kernel_norm / (smoothing * smoothing)
eos_stiff = sound_speed * sound_speed / 7.0
particle_mass = 0.125
viscosity = 0.1
visc_floor = 0.01 * smoothing * smoothing
time_step = 0.01
gravity = 9.81
layer_block = 4


def extended_2(block, sides, width):
    for axis, dim in sides:
        count = lax.axis_size(axis)
        forward = [(i, i + 1) for i in range(count - 1)]
        backward = [(target, source) for source, target in forward]
        low = lax.ppermute(
            lax.slice_in_dim(block, block.shape[dim] - width, None, axis=dim), axis, forward
        )
        high = lax.ppermute(lax.slice_in_dim(block, 0, width, axis=dim), axis, backward)
        block = jnp.concatenate([low, block, high], axis=dim)
    return block


def shifted(value, axis, steps):
    count = lax.axis_size(axis)
    leading, last = (max(0, -steps), min(count, count - steps))
    return lax.ppermute(value, axis, [(source, source + steps) for source in range(leading, last)])


def occupied(cell_counts):
    filled = jnp.repeat(cell_counts, SLOTS, axis=-1)
    slot_index = jnp.arange(filled.shape[-1], dtype=jnp.int32) % SLOTS
    return (slot_index < filled).astype(jnp.float32)


def pair_rates(center, beside_all):
    span_x, span_y, span_z = (center.shape[1], center.shape[2], center.shape[3])
    dens_c = center[6] + 1.0 - center[7]
    dens_n = beside_all[6] + 1.0 - beside_all[7]
    ratio_c = eos_stiff * (dens_c**7 - 1.0) / (dens_c * dens_c)
    ratio_n = eos_stiff * (dens_n**7 - 1.0) / (dens_n * dens_n)
    accel_sum = jnp.zeros((3,) + center.shape[1:], jnp.float32)
    drift_sum = jnp.zeros(center.shape[1:], jnp.float32)
    for step_x in range(3):
        for step_y in range(3):
            for step_z in range(3):
                neighbour = beside_all[
                    :, step_x : step_x + span_x, step_y : step_y + span_y, step_z : step_z + span_z
                ]
                near_dens = dens_n[
                    step_x : step_x + span_x, step_y : step_y + span_y, step_z : step_z + span_z
                ]
                near_ratio = ratio_n[
                    step_x : step_x + span_x, step_y : step_y + span_y, step_z : step_z + span_z
                ]
                cell_gap = (
                    jnp.array(
                        [float(1 - step_x), float(1 - step_y), float(1 - step_z)], jnp.float32
                    ).reshape(3, 1, 1, 1, 1, 1)
                    * cell_side
                )
                offset_vec = center[0:3, ..., None] - neighbour[0:3, ..., None, :] + cell_gap
                dist_sq = jnp.sum(offset_vec * offset_vec, axis=0)
                support = jnp.maximum(1.0 - jnp.sqrt(dist_sq) / (2.0 * smoothing), 0.0)
                slope_term = grad_scale * support * support * support * neighbour[7][..., None, :]
                approach = jnp.sum(
                    (center[3:6, ..., None] - neighbour[3:6, ..., None, :]) * offset_vec, axis=0
                )
                mean_dens = 0.5 * (dens_c[..., None] + near_dens[..., None, :])
                visc_term = (
                    -viscosity
                    * sound_speed
                    * smoothing
                    * jnp.minimum(approach, 0.0)
                    / ((dist_sq + visc_floor) * mean_dens)
                )
                force_term = (
                    ratio_c[..., None] + near_ratio[..., None, :] + visc_term
                ) * slope_term
                accel_sum = accel_sum - particle_mass * jnp.sum(force_term * offset_vec, axis=-1)
                drift_sum = drift_sum + particle_mass * jnp.sum(slope_term * approach, axis=-1)
    gravity_vec = jnp.array([0.0, 0.0, gravity], jnp.float32).reshape(3, 1, 1, 1, 1)
    return jnp.concatenate([accel_sum - gravity_vec, drift_sum[None]], axis=0)


def region_rates(extended):
    span_x = extended.shape[1] - 2
    span_y = extended.shape[2] - 2
    layers = extended.shape[3] // SLOTS
    cells_grid = extended.reshape(8, span_x + 2, span_y + 2, layers, SLOTS)
    padded = jnp.pad(cells_grid, ((0, 0), (0, 0), (0, 0), (1, 1), (0, 0)))

    def one_block(block_index):
        layer_start = block_index * layer_block
        beside_all = lax.dynamic_slice_in_dim(padded, layer_start, layer_block + 2, axis=3)
        return pair_rates(beside_all[:, 1:-1, 1:-1, 1:-1], beside_all)

    stacked = lax.map(one_block, jnp.arange(layers // layer_block, dtype=jnp.int32))
    ordered = jnp.moveaxis(stacked, 0, 3)
    return ordered.reshape(4, span_x, span_y, layers * SLOTS)


def predict(fields, rates_now):
    position = fields[0:3] + 0.5 * time_step * fields[3:6]
    velocity = fields[3:6] + 0.5 * time_step * rates_now[0:3]
    density = fields[6:7] + 0.5 * time_step * rates_now[3:4]
    return jnp.concatenate([position, velocity, density, fields[7:8]], axis=0)


def correct(fields, rates_mid):
    velocity = fields[3:6] + time_step * rates_mid[0:3]
    density = fields[6:7] + time_step * rates_mid[3:4]
    position = fields[0:3] + 0.5 * time_step * (fields[3:6] + velocity)
    return jnp.concatenate([position, velocity, density], axis=0)


def pack_leavers(face_state, face_count, face_leave):
    cell_total = face_count.shape[0] * face_count.shape[1]
    row_total = cell_total * LMAX // 2
    leave_quota = face_leave.reshape(cell_total)
    occupancy = face_count.reshape(cell_total)
    row_ends = jnp.cumsum(leave_quota, dtype=jnp.int32)
    starts = row_ends - leave_quota
    row_ids = jnp.arange(row_total, dtype=jnp.int32)
    owner_mask = (starts[None, :] <= row_ids[:, None]) & (row_ends[None, :] > row_ids[:, None])
    root = jnp.arange(cell_total, dtype=jnp.int32) * SLOTS + occupancy - leave_quota - starts
    source_row = jnp.sum(jnp.where(owner_mask, root[None, :], 0), axis=1, dtype=jnp.int32) + row_ids
    flat_face = face_state.reshape(7, cell_total * SLOTS)
    return jnp.take(flat_face, source_row, axis=1)


def shards(particles, counts, leavers):
    size_x = particles.shape[1]
    fields = jnp.concatenate([particles, occupied(counts)[None]], axis=0)
    current = fields
    for section_no in range(2):
        rates_now = region_rates(extended_2(current, (("slab", 1), ("tile", 2)), 1))
        if section_no == 0:
            current = predict(fields, rates_now)
    updated = correct(fields, rates_now)
    remain = counts.at[0].add(-leavers[0, 0]).at[size_x - 1].add(-leavers[1, 0])
    kept = updated * occupied(remain)[None]
    lower_rows = pack_leavers(updated[:, 0], counts[0], leavers[0, 0])
    upper_rows = pack_leavers(updated[:, size_x - 1], counts[size_x - 1], leavers[1, 0])
    from_below = shifted(upper_rows, "slab", 1)
    from_above = shifted(lower_rows, "slab", -1)
    return (kept, jnp.stack([from_below, from_above], axis=0))


def solution(mesh):
    return jax.shard_map(
        shards,
        mesh=mesh,
        in_specs=(
            P(None, "slab", "tile", None),
            P("slab", "tile", None),
            P(None, "slab", "tile", None),
        ),
        out_specs=(P(None, "slab", "tile", None), P(None, None, ("slab", "tile"))),
        check_vma=False,
    )
```

profile of v0, /device:TPU:10, one launch (start us, length us, event | category | flops | bytes accessed | tf_op | source)
XLA Modules:
  0.0 1146.7 jit_solution(4645986257113865768)
XLA Ops:
  2.6 4.2 collective-permute-start
  6.8 4.0 collective-permute-start.1
  19.6 5.8 collective-permute-start.3
  37.0 525.1 %while.30 = (s32[]{:T(128)}, f32[12,4,2,2,4,32]{5,4,3,2,1,0:T(4,128)}, s32[12]{0:T(128)}, f32[8,4,4,50,32]{4,3,0,2,1:T(8,128)}, s32[]{:T(128)}, /*index=5*/f32[3...) while((s32[]{:T(128)}, ...), condition=%wide.region_109.110_spmd.clone, body=%wide.region_0.109_spmd.sunk.clone.sunk | while | flops 21704204 | bytes 16404091 | solution.py:113
  39.1 5.0 constant_dynamic-slice_fusion.166
  44.2 3.7 multiply_reduce_fusion.237
  83.0 5.0 constant_dynamic-slice_fusion.166
  88.1 3.7 multiply_reduce_fusion.237
  126.9 5.0 constant_dynamic-slice_fusion.166
  132.0 3.7 multiply_reduce_fusion.237
  170.6 5.0 constant_dynamic-slice_fusion.166
  175.7 3.7 multiply_reduce_fusion.237
  214.2 4.7 constant_dynamic-slice_fusion.166
  219.0 3.7 multiply_reduce_fusion.237
  257.6 4.7 constant_dynamic-slice_fusion.166
  262.4 3.7 multiply_reduce_fusion.237
  301.0 5.0 constant_dynamic-slice_fusion.166
  306.1 3.7 multiply_reduce_fusion.237
  344.7 5.0 constant_dynamic-slice_fusion.166
  349.8 3.7 multiply_reduce_fusion.237
  388.4 5.0 constant_dynamic-slice_fusion.166
  393.5 3.7 multiply_reduce_fusion.237
  432.2 5.0 constant_dynamic-slice_fusion.166
  437.3 3.7 multiply_reduce_fusion.237
  476.1 5.1 constant_dynamic-slice_fusion.166
  481.3 3.7 multiply_reduce_fusion.237
  519.9 5.1 constant_dynamic-slice_fusion.166
  570.7 4.8 collective-permute-start.5
  581.9 5.8 collective-permute-start.7
  598.4 525.1 %while.31 = (s32[]{:T(128)}, f32[12,4,2,2,4,32]{5,4,3,2,1,0:T(4,128)}, s32[12]{0:T(128)}, f32[8,4,4,50,32]{4,3,0,2,1:T(8,128)}, s32[]{:T(128)}, /*index=5*/f32[3...) while((s32[]{:T(128)}, ...), condition=%wide.region_219.220_spmd.clone, body=%wide.region_110.219_spmd.sunk.clone.sunk | while | flops 21704204 | bytes 16404091 | solution.py:113
  600.6 5.0 constant_dynamic-slice_fusion.167
  644.5 5.0 constant_dynamic-slice_fusion.167
  649.6 3.7 multiply_reduce_fusion.249
  688.4 5.0 constant_dynamic-slice_fusion.167
  693.5 3.7 multiply_reduce_fusion.249
  732.1 5.0 constant_dynamic-slice_fusion.167
  775.8 4.6 constant_dynamic-slice_fusion.167
  819.2 4.6 constant_dynamic-slice_fusion.167
  862.7 5.0 constant_dynamic-slice_fusion.167
  906.4 5.0 constant_dynamic-slice_fusion.167
  950.1 4.9 constant_dynamic-slice_fusion.167
  955.1 3.7 multiply_reduce_fusion.249
  994.0 4.9 constant_dynamic-slice_fusion.167
  999.0 3.7 multiply_reduce_fusion.249
  1037.9 5.0 constant_dynamic-slice_fusion.167
  1081.7 5.0 constant_dynamic-slice_fusion.167
  1130.7 5.7 collective-permute-start.8
  1140.5 5.4 collective-permute-done.9
  (5775 shorter events, 878.9 us)
Async XLA Ops:
  1.5 28.5 %copy-start.112 = (f32[1,2,2,1536]{3,2,1,0:T(2,128)}, f32[1,2,2,1536]{3,2,1,0:T(2,128)S(1)}, u32[]{:S(2)}) copy-start(f32[1,2,2,1536]{3,2,1,0:T(2,128)S(1)} %compare_convert_fusion.1) | copy-start | bytes 73732
  2.6 13.7 %collective-permute-start = (f32[8,1,2,1536]{3,2,1,0:T(2,128)S(1)}, f32[8,1,2,1536]{3,2,1,0:T(2,128)S(1)}, u32[]{:S(2)}, u32[]{:S(2)}) collective-permute-start(f32[8,1,2,1536]{3,2,1,0:T(2,128)S(1)} %get-tuple-element.1855), channel_id=1, source_target_pairs={{0,16},{16,32},{32,48},{48,64},{64,80},{80,96},{96,112},{1,17},{17... | collective-permute-start | bytes 294920 | tf_op jit(solution)/shard_map/ppermute | solution.py:31
  6.8 9.5 collective-permute-start.1
  15.1 14.9 %copy-start.210 = (s32[192]{0:T(256)}, s32[192]{0:T(256)S(1)}, u32[]{:S(2)}) copy-start(s32[192]{0:T(256)S(1)} %select_reduce_fusion) | copy-start | bytes 2308
  17.7 9.1 collective-permute-start.2
  19.6 8.9 collective-permute-start.3
  39.0 8.9 copy-start.160
  39.1 8.9 copy-start.166
  39.1 8.9 copy-start.172
  39.1 8.9 copy-start.176
  82.9 8.9 copy-start.160
  82.9 8.9 copy-start.166
  82.9 8.9 copy-start.172
  300.9 8.9 copy-start.160
  301.0 8.9 copy-start.166
  301.0 8.9 copy-start.172
  344.6 8.9 copy-start.160
  344.6 8.9 copy-start.166
  344.7 8.9 copy-start.172
  476.0 9.0 copy-start.160
  476.0 9.0 copy-start.166
  476.1 9.0 copy-start.172
  476.1 9.0 copy-start.176
  476.1 9.0 copy-start.180
  519.8 9.0 copy-start.160
  519.8 9.0 copy-start.166
  519.8 9.0 copy-start.172
  519.8 9.0 copy-start.176
  519.9 9.0 copy-start.180
  562.1 25.6 %copy-start.211 = (s32[192]{0:T(256)S(1)}, s32[192]{0:T(256)}, u32[]{:S(2)}) copy-start(s32[192]{0:T(256)} %copy-done.210) | copy-start | bytes 2308
  562.1 28.7 %copy-start.113 = (f32[1,2,2,1536]{3,2,1,0:T(2,128)S(1)}, f32[1,2,2,1536]{3,2,1,0:T(2,128)}, u32[]{:S(2)}) copy-start(f32[1,2,2,1536]{3,2,1,0:T(2,128)} %copy-done.112) | copy-start | bytes 73732
  567.2 9.5 collective-permute-start.4
  570.7 8.0 collective-permute-start.5
  580.0 9.1 collective-permute-start.6
  581.9 8.9 collective-permute-start.7
  1037.8 8.9 copy-start.162
  1037.8 8.9 copy-start.168
  1037.8 8.9 copy-start.174
  1037.8 8.9 copy-start.178
  1037.8 8.9 copy-start.182
  1081.6 8.9 copy-start.162
  1081.6 8.9 copy-start.168
  1081.6 8.9 copy-start.174
  1081.6 8.9 copy-start.178
  1081.6 8.9 copy-start.182
  1123.5 14.2 %copy-start.213 = (pred[192]{0:T(512)(128)(4,1)S(1)}, pred[192]{0:T(512)(128)(4,1)}, u32[]{:S(2)}) copy-start(pred[192]{0:T(512)(128)(4,1)} %compare_and_fusion) | copy-start | bytes 580
  1130.7 9.7 collective-permute-start.8
  1137.8 8.0 collective-permute-start.9
  (2464 other events, 11981.7 us)
where the time goes:
time: 1160 us; the launch traced here: 1150 us
  other arithmetic  793 us (68%)
  local copies, waits for them, and re-layouts  243 us (21%)
  loops' own time  57 us (5%)
  starting transfers between devices  40.1 us (3%)
  waiting for transfers between devices  12.7 us (1%)
    reduce_sum x120, other arithmetic, pair_rates(): jnp.sum(force_term * offset_vec, axis=-1)  259 us
    reduce_sum x120, other arithmetic, pair_rates(): dist_sq = jnp.sum(offset_vec * offset_vec, axis=0)  225 us
    mul x168, other arithmetic, pair_rates(): (ratio_c[..., None] + near_ratio[..., None, :] + visc_term) * slope_term  177 us
    slice x24, local copies, waits for them, and re-layouts, pair_rates(): neighbour[3:6, ..., None, :]  119 us
    mul x24, local copies, waits for them, and re-layouts, pair_rates(): grad_scale * support * support * support * neighbour[7][..., None, :]  60.5 us
    another operation x2, loops' own time, region_rates(): lax.map(one_block, jnp.arange(layers // layer_block, dtype=jnp.int32))  57 us
    reduce_sum x48, other arithmetic, pair_rates(): jnp.sum(slope_term * approach, axis=-1)  43.6 us
    dynamic_slice x24, local copies, waits for them, and re-layouts, region_rates(): lax.map(one_block, jnp.arange(layers // layer_block, dtype=jnp.int32))  29.4 us

commit v1 on v0

v1 whole, which is shorter than its diff:
```python
import math

import jax
import jax.numpy as jnp
from jax import lax
from jax.experimental import pallas as pl
from jax.experimental.pallas import tpu as pltpu
from jax.sharding import PartitionSpec as P

SLOTS = 32
LMAX = 4
CZ = 48
BLOCKS = 12

sound_speed = 10.0
smoothing = 0.5
kernel_norm = 21.0 / (16.0 * math.pi * smoothing**3)
grad_scale = -5.0 * kernel_norm / (smoothing * smoothing)
eos_stiff = sound_speed * sound_speed / 7.0
particle_mass = 0.125
viscosity = 0.1
visc_floor = 0.01 * smoothing * smoothing
time_step = 0.01
gravity = 9.81
mass_grad = particle_mass * grad_scale
visc_gain = 2.0 * viscosity * sound_speed * smoothing
FAR = 1e15

OWN = [(0, 0), (0, 1), (1, 0), (1, 1)]


def column_rows(src, far_x, far_y, col, lhs):
    sub = lax.broadcasted_iota(jnp.int32, (8, 128), 0)
    shift = jnp.where(sub == 0, far_x, jnp.where(sub == 1, far_y, 0.0))
    high, mid, low = [], [], []
    for r in range(BLOCKS):
        vals = src[r]
        absent = jnp.broadcast_to(vals[6:7], (8, 128)) == 0.0
        vals = jnp.where((sub == 0) & absent, FAR, vals + shift)
        top = vals.astype(jnp.bfloat16).astype(jnp.float32)
        rest = vals - top
        second = rest.astype(jnp.bfloat16).astype(jnp.float32)
        high.append(top)
        mid.append(second)
        low.append(rest - second)
    pairs = [jnp.where(sub < 4, low[r], pltpu.roll(low[r + 6], 4, 0)) for r in range(6)]
    zero = jnp.zeros((8, 128), jnp.float32)
    first = jnp.concatenate(high + pairs[:4], axis=0)
    second = jnp.concatenate(mid + pairs[4:] + [zero, zero], axis=0)
    rows = pl.ds(pl.multiple_of(col * 128, 128), 128)
    lhs[rows, 0:128] = first.T.astype(jnp.bfloat16)
    lhs[rows, 128:256] = second.T.astype(jnp.bfloat16)


def select_matrix():
    k = lax.broadcasted_iota(jnp.int32, (256, 3072), 0)
    n = lax.broadcasted_iota(jnp.int32, (256, 3072), 1)
    local, sub = k % 128, k % 8
    whole = local < 96
    pair_row = (local - 96) // 8 + jnp.where(k < 128, 0, 4)
    field = jnp.where(whole, sub, sub % 4)
    row = jnp.where(whole, local // 8, pair_row + 6 * (sub // 4))
    row = jnp.where(k < 240, row, -1)
    want_field, beta, chunk = n // 384, (n // 128) % 3, (n % 128) // 32
    return ((field == want_field) & (row == 3 * chunk + beta)).astype(jnp.bfloat16)


def spread_columns(count, lhs, select, tiles, first):
    level = lax.broadcasted_iota(jnp.int32, (16, 8, 128), 0) // 4

    def two(n, _):
        rows = lhs[pl.ds(pl.multiple_of(n * 256, 256), 256), :]
        for t in range(12):
            out = jnp.dot(rows, select[:, 256 * t:256 * t + 256],
                          preferred_element_type=jnp.float32)
            for h in range(2):
                f, beta = (2 * t + h) // 3, (2 * t + h) % 3
                for m in range(2):
                    part = out[128 * m:128 * m + 128, 128 * h:128 * h + 128].reshape(16, 8, 128)
                    if f == 2:
                        part = part + (level + 4 * beta).astype(jnp.float32)
                    tiles[first + 2 * n + m, f, 16 * beta + 4:16 * beta + 20] = part
        return 0
    lax.fori_loop(0, count // 2, two, 0)
    chunk = lax.broadcasted_iota(jnp.int32, (8, 128), 1) // 32

    def edges(c, _):
        for s in range(4):
            for f in range(8):
                below = pltpu.roll(tiles[first + c, f, 48 + s], 32, 1)
                above = pltpu.roll(tiles[first + c, f, 4 + s], 96, 1)
                if f == 0:
                    below = jnp.where(chunk == 0, FAR, below)
                    above = jnp.where(chunk == 3, FAR, above)
                if f == 2:
                    below = below - 12.0
                    above = above + 12.0
                tiles[first + c, f, s] = below
                tiles[first + c, f, 52 + s] = above
        return 0
    lax.fori_loop(0, count, edges, 0)


def swap_chunks(load, store):
    chunk = lax.broadcasted_iota(jnp.int32, (8, 128), 1) // 32
    for beta in range(3):
        rows = [load(3 * g + beta) for g in range(4)]
        for q in range(4):
            res = rows[q]
            for g in range(4):
                if g != q:
                    res = jnp.where(chunk == g, pltpu.roll(rows[g], (32 * (g - q)) % 128, 1), res)
            store(4 * beta + q, res)


def swap_back(load, store):
    chunk = lax.broadcasted_iota(jnp.int32, (8, 128), 1) // 32
    for beta in range(3):
        rows = [load(4 * beta + q) for q in range(4)]
        for g in range(4):
            res = rows[g]
            for q in range(4):
                if g != q:
                    res = jnp.where(chunk == q, pltpu.roll(rows[q], (32 * (q - g)) % 128, 1), res)
            store(3 * g + beta, res)


def pair(acc, center, tile):
    xi, yi, zi, ui, vi, wi, di, ri = center
    dx = xi - tile[0]
    dy = yi - tile[1]
    dz = zi - tile[2]
    r2 = dx * dx + dy * dy + dz * dz
    approach = (tile[3] - ui) * dx + (tile[4] - vi) * dy + (tile[5] - wi) * dz
    dist = r2 * lax.rsqrt(jnp.maximum(r2, 1e-30))
    support = jnp.maximum(1.0 - dist, 0.0)
    slope = support * support * support
    visc = jnp.maximum(approach, 0.0) / ((r2 + visc_floor) * (di + tile[6]))
    force = (ri + tile[7] + visc) * slope
    return (acc[0] + force * dx, acc[1] + force * dy, acc[2] + force * dz,
            acc[3] + slope * approach)


def center_rows(rows, far_x, far_y, b):
    vals = [jnp.broadcast_to(rows[f:f + 1, :], (8, 128)) for f in range(8)]
    vals[0] = vals[0] + far_x
    vals[1] = vals[1] + far_y
    vals[2] = vals[2] + b.astype(jnp.float32)
    return vals


def center_blocks(own, blocks):
    def one(c, _):
        swap_chunks(lambda r: own[c, r], lambda r, v: blocks.__setitem__((c, r), v))
        return 0
    lax.fori_loop(0, 4, one, 0)


def all_pairs(blocks, tiles, neighbours, emit):
    def sums_at(c, cx, cy, b, js):
        center = center_rows(blocks[c, b], cx, cy, b)
        acc = tuple(jnp.zeros((8, 128), jnp.float32) for _ in range(4))
        for j in js:
            for d in range(3):
                for s in range(4):
                    acc = pair(acc, center, [tiles[j, f, (b + d) * 4 + s] for f in range(8)])
        emit(c, b, jnp.concatenate([jnp.sum(a, axis=0, keepdims=True) for a in acc]
                                   + [jnp.zeros((4, 128), jnp.float32)], axis=0))

    for c, (cx, cy) in enumerate(OWN):
        def step(b, _, c=c, cx=cx, cy=cy):
            sums_at(c, float(cx), float(cy), b, neighbours(cx, cy))
            return 0
        lax.fori_loop(0, BLOCKS, step, 0)


def near_kernel(own, select, acc_out, blocks, lhs, tiles):
    center_blocks(own, blocks)
    for c, (x, y) in enumerate(OWN):
        column_rows(own.at[c], float(x), float(y), c, lhs)
    spread_columns(4, lhs, select, tiles, 0)

    def emit(c, b, sums):
        acc_out[c, b] = sums
    all_pairs(blocks, tiles, lambda cx, cy: range(4), emit)


def slab_kernel(own, acc_in, low, high, select, acc_out, blocks, lhs, tiles):
    center_blocks(own, blocks)
    for n, (ref, x) in enumerate(((low, -1.0), (high, 2.0))):
        for y in range(2):
            column_rows(ref.at[y], x, float(y), 2 * n + y, lhs)
    spread_columns(4, lhs, select, tiles, 0)

    def emit(c, b, sums):
        acc_out[c, b] = sums + acc_in[c, b]
    all_pairs(blocks, tiles, lambda cx, cy: (2 * cx, 2 * cx + 1), emit)


def tile_kernel(final, base, own, acc_in, low, high, select, out, blocks, lhs, tiles, res):
    center_blocks(own, blocks)

    for n, (ref, y) in enumerate(((low, -1.0), (high, 2.0))):
        def one(i, _, n=n, ref=ref, y=y):
            column_rows(ref.at[i], (i - 1).astype(jnp.float32), y, 4 * n + i, lhs)
            return 0
        lax.fori_loop(0, 4, one, 0)
    spread_columns(8, lhs, select, tiles, 0)

    def emit(c, b, sums):
        res[c, b] = sums + acc_in[c, b]
    all_pairs(blocks, tiles, lambda cx, cy: range(4 * cy + cx, 4 * cy + cx + 3), emit)

    def finish(c, _):
        def store(r, rates):
            now = base[c, r]
            present = now[6:7] != 0.0
            ax = -mass_grad * rates[0:1]
            ay = -mass_grad * rates[1:2]
            az = -mass_grad * rates[2:3] - gravity
            drift = -mass_grad * rates[3:4]
            half = 0.5 * time_step
            if not final:
                dens = now[6:7] + half * drift
                dens = jnp.where(present, dens, 1.0)
                ratio = eos_stiff * (dens**7 - 1.0) / (dens * dens)
                vals = [now[0:1] + half * now[3:4], now[1:2] + half * now[4:5],
                        now[2:3] + half * now[5:6], now[3:4] + half * ax,
                        now[4:5] + half * ay, now[5:6] + half * az, dens, ratio]
            else:
                v1 = [now[3:4] + time_step * ax, now[4:5] + time_step * ay,
                      now[5:6] + time_step * az]
                vals = [now[k:k + 1] + half * (now[3 + k:4 + k] + v1[k]) for k in range(3)]
                vals += v1 + [now[6:7] + time_step * drift, now[7:8]]
            full = jnp.concatenate(vals, axis=0)
            out[c, r] = jnp.where(jnp.broadcast_to(present, (8, 128)), full, 0.0)
        swap_back(lambda r: res[c, r], store)
        return 0
    lax.fori_loop(0, 4, finish, 0)


def pair_call(body, name, columns, args, extra=()):
    return pl.pallas_call(
        body,
        out_shape=jax.ShapeDtypeStruct((4, BLOCKS, 8, 128), jnp.float32),
        scratch_shapes=[pltpu.VMEM((4, BLOCKS, 8, 128), jnp.float32),
                        pltpu.VMEM((columns * 128, 256), jnp.bfloat16),
                        pltpu.VMEM((columns, 8, 4 * BLOCKS + 8, 8, 128), jnp.float32),
                        *extra],
        compiler_params=pltpu.CompilerParams(vmem_limit_bytes=40 << 20),
        name=name,
    )(*args)


def rates_pass(final, base, own, select):
    low = shifted(own[2:4], "slab", 1)
    high = shifted(own[0:2], "slab", -1)
    acc = pair_call(near_kernel, "near_pairs", 4, (own, select))
    front = shifted(jnp.concatenate([low[1:2], own[1:2], own[3:4], high[1:2]]), "tile", 1)
    back = shifted(jnp.concatenate([low[0:1], own[0:1], own[2:3], high[0:1]]), "tile", -1)
    acc = pair_call(slab_kernel, "slab_pairs", 4, (own, acc, low, high, select))

    def body(*refs):
        tile_kernel(final, *refs)
    return pair_call(body, "tile_pairs_final" if final else "tile_pairs", 8,
                     (base, own, acc, front, back, select),
                     (pltpu.VMEM((4, BLOCKS, 8, 128), jnp.float32),))


def slot_mask(cell_counts):
    slot = lax.broadcasted_iota(jnp.int32, cell_counts.shape + (SLOTS,), cell_counts.ndim)
    return slot < cell_counts[..., None]


def pack_leavers(face_state, face_count, face_leave):
    cell_total = face_count.shape[0] * face_count.shape[1]
    row_total = cell_total * LMAX // 2
    leave_quota = face_leave.reshape(cell_total)
    occupancy = face_count.reshape(cell_total)
    row_ends = jnp.cumsum(leave_quota, dtype=jnp.int32)
    starts = row_ends - leave_quota
    row_ids = jnp.arange(row_total, dtype=jnp.int32)
    owner_mask = (starts[None, :] <= row_ids[:, None]) & (row_ends[None, :] > row_ids[:, None])
    root = jnp.arange(cell_total, dtype=jnp.int32) * SLOTS + occupancy - leave_quota - starts
    source_row = jnp.sum(jnp.where(owner_mask, root[None, :], 0), axis=1, dtype=jnp.int32) + row_ids
    flat_face = face_state.reshape(7, cell_total * SLOTS)
    return jnp.take(flat_face, source_row, axis=1)


def shifted(value, axis, steps):
    count = lax.axis_size(axis)
    leading, last = (max(0, -steps), min(count, count - steps))
    return lax.ppermute(value, axis, [(source, source + steps) for source in range(leading, last)])


def start_fields(particles, counts):
    mask = slot_mask(counts).reshape(2, 2, CZ * SLOTS)
    dens = jnp.where(mask, particles[6], 1.0)
    ratio = eos_stiff * (dens**7 - 1.0) / (dens * dens)
    fields = jnp.concatenate([particles, ratio[None]], axis=0)
    fields = jnp.where(mask[None], fields, 0.0)
    return fields.reshape(8, 4, BLOCKS, 128).transpose(1, 2, 0, 3)


def finish_fields(updated):
    return updated.transpose(2, 0, 1, 3)[:7].reshape(7, 2, 2, CZ * SLOTS)


def shards(particles, counts, leavers):
    fields = start_fields(particles, counts)
    select = select_matrix()
    middle = rates_pass(False, fields, fields, select)
    updated = finish_fields(rates_pass(True, fields, middle, select))
    remain = counts.at[0].add(-leavers[0, 0]).at[1].add(-leavers[1, 0])
    kept = jnp.where(slot_mask(remain).reshape(1, 2, 2, CZ * SLOTS), updated, 0.0)
    lower_rows = pack_leavers(updated[:, 0], counts[0], leavers[0, 0])
    upper_rows = pack_leavers(updated[:, 1], counts[1], leavers[1, 0])
    from_below = shifted(upper_rows, "slab", 1)
    from_above = shifted(lower_rows, "slab", -1)
    return (kept, jnp.stack([from_below, from_above], axis=0))


def solution(mesh):
    return jax.shard_map(
        shards,
        mesh=mesh,
        in_specs=(
            P(None, "slab", "tile", None),
            P("slab", "tile", None),
            P(None, "slab", "tile", None),
        ),
        out_specs=(P(None, "slab", "tile", None), P(None, None, ("slab", "tile"))),
        check_vma=False,
    )
```

time: 1160 us -> 139 us (0.12)
  other arithmetic: 793 us -> 4.71 us
  local copies, waits for them, and re-layouts: 243 us -> 5.85 us
  Pallas kernels: 0 us -> 79.5 us
  loops' own time: 57 us -> 0 us
    reduce_sum x288 -> x0, other arithmetic: 528 us -> none  [the longest x120 259 us: pair_rates(): jnp.sum(force_term * offset_vec, axis=-1)]
    mul x173 -> x0, other arithmetic: 182 us -> none  [the longest x168 177 us: pair_rates(): (ratio_c[..., None] + near_ratio[..., None, :] + visc_term) * slope_term]
    slice x102 -> x12, local copies, waits for them, and re-layouts: 122 us -> 0.64 us  [the longest x2 0.51 us: shards(): upper_rows = pack_leavers(updated[:, 1], counts[1], leavers[1, 0])]
    pallas_call x0 -> x6, Pallas kernels: none -> 79.5 us  [pair_call(): pl.pallas_call(body, out_shape=jax.ShapeDtypeStruct((4, BLOCKS, 8, 128),...]
    mul x32 -> x0, local copies, waits for them, and re-layouts: 61.4 us -> none  [the longest x24 60.5 us: pair_rates(): grad_scale * support * support * support * neighbour[7][..., None, :]]
    another operation x2 -> x0, loops' own time: 57 us -> none  [region_rates(): lax.map(one_block, jnp.arange(layers // layer_block, dtype=jnp.int32))]
    div x48 -> x3, other arithmetic: 47.1 us -> 0.79 us  [the longest x1 0.78 us: start_fields(): ratio = eos_stiff * (dens ** 7 - 1.0) / (dens * dens)]
    ppermute x8 -> x0, starting transfers between devices: 31.8 us -> none  [the longest x4 20.3 us: extended_2(): lax.ppermute(lax.slice_in_dim(block, 0, width, axis=dim), axis, backward)]
where the time goes in v1:
time: 139 us; the launch traced here: 137 us
  Pallas kernels  79.5 us (57%)
  starting transfers between devices  38.5 us (28%)
  waiting for transfers between devices  7.49 us (5%)
  local copies, waits for them, and re-layouts  5.85 us (4%)
  other arithmetic  4.71 us (3%)
    pallas_call x6, Pallas kernels, pair_call(): pl.pallas_call(body, out_shape=jax.ShapeDtypeStruct((4, BLOCKS, 8, 128),...  79.5 us
    ppermute x10, starting transfers between devices, shifted(): lax.ppermute(value, axis, [(source, source + steps) for source in range(l...  38.5 us
    ppermute x10, waiting for transfers between devices, shifted(): lax.ppermute(value, axis, [(source, source + steps) for source in range(l...  7.49 us
  transfers between devices with their start and end apart: 10, of which 3 were waited for; matrix products, arithmetic and copies ran while one was open for 4% of the time, Pallas kernels for 36%

profile of v1, /device:TPU:10, one launch (start us, length us, event | category | flops | bytes accessed | tf_op | source)
XLA Modules:
  0.0 137.2 jit_solution(1295437639259495980)
XLA Ops:
  0.6 0.7 copy.36
  1.4 0.1 lt.169
  1.5 0.1 lt.167
  1.7 1.1 concatenate.24
  2.8 0.8 multiply_divide_fusion
  3.6 0.1 copy.25
  3.9 4.2 %collective-permute-start = (f32[2,12,8,128]{3,2,1,0:T(8,128)S(1)}, f32[2,12,8,128]{3,2,1,0:T(8,128)S(1)}, u32[]{:S(2)}, u32[]{:S(2)}) collective-permute-start(f32[2,12,8,128]{3,2,1,0:T(8,128)S(1)} %get-tuple-element.46), channel_id=1, source_target_pairs={{0,16},{16,32},{32,48},{48,64},{64,80},{80,96},{96,112},{1,17},{17... | collective-permute-start | bytes 294920 | tf_op jit(solution)/shard_map/ppermute | solution.py:293
  8.1 4.0 %collective-permute-start.1 = (f32[2,12,8,128]{3,2,1,0:T(8,128)S(1)}, f32[2,12,8,128]{3,2,1,0:T(8,128)S(1)}, u32[]{:S(2)}, u32[]{:S(2)}) collective-permute-start(f32[2,12,8,128]{3,2,1,0:T(8,128)S(1)} %get-tuple-element.45), channel_id=1, source_target_pairs={{16,0},{32,16},{48,32},{64,48},{80,64},{96,80},{112,96},{17,1},{33... | collective-permute-start | bytes 294920 | tf_op jit(solution)/shard_map/ppermute | solution.py:293
  12.3 0.1 reshape_squeeze.22
  12.4 0.1 reshape.249
  12.5 0.1 reshape_squeeze.19
  12.6 0.1 reshape.248
  12.8 1.3 fusion.36.select.refs_5_
  14.1 15.2 %near_pairs.2.acc_in = f32[4,12,8,128]{3,2,1,0:T(8,128)S(1)} custom-call(f32[4,12,8,128]{3,2,1,0:T(8,128)S(1)} %fusion.37.own.refs_0_.refs_1_, bf16[256,3072]{1,0:T(8,128)(2,1)S(1)} %fusion.36.select.refs_5_), custom_call_target="tpu_custom_call" | custom-call | tf_op jit(solution)/shard_map/near_pairs/pallas_call | solution.py:243
  29.4 0.1 lt.164
  29.6 0.1 reshape_squeeze.23
  29.6 0.1 reduce-window.15
  29.8 0.1 reduce.5
  29.9 0.1 select_reduce_fusion
  30.0 0.1 reshape_squeeze.20
  30.1 0.1 reduce-window.14
  30.3 0.1 reduce.4
  30.4 0.1 select_reduce_fusion.1
  30.6 1.9 %collective-permute-start.2 = (f32[4,12,8,128]{3,2,1,0:T(8,128)S(1)}, f32[4,12,8,128]{3,2,1,0:T(8,128)S(1)}, u32[]{:S(2)}, u32[]{:S(2)}) collective-permute-start(f32[4,12,8,128]{3,2,1,0:T(8,128)S(1)} %pad_maximum_fusion), channel_id=1, source_target_pairs={{0,1},{1,2},{2,3},{3,4},{4,5},{5,6},{6,7},{7,8},{8,9},{9,10},{10,1... | collective-permute-start | bytes 589832 | tf_op jit(solution)/shard_map/ppermute | solution.py:293
  32.6 5.8 %collective-permute-start.3 = (f32[4,12,8,128]{3,2,1,0:T(8,128)S(1)}, f32[4,12,8,128]{3,2,1,0:T(8,128)S(1)}, u32[]{:S(2)}, u32[]{:S(2)}) collective-permute-start(f32[4,12,8,128]{3,2,1,0:T(8,128)S(1)} %pad_maximum_fusion.1), channel_id=1, source_target_pairs={{1,0},{2,1},{3,2},{4,3},{5,4},{6,5},{7,6},{8,7},{9,8},{10,9},{11,1... | collective-permute-start | bytes 589832 | tf_op jit(solution)/shard_map/ppermute | solution.py:293
  38.3 9.3 %slab_pairs.2.refs_2_ = f32[4,12,8,128]{3,2,1,0:T(8,128)S(1)} custom-call(f32[4,12,8,128]{3,2,1,0:T(8,128)S(1)} %fusion.37.own.refs_0_.refs_1_, f32[4,12,8,128]{3,2,1,0:T(8,128)S(1)} %near_pairs.2.acc_in, f32[2,12,8,128]{3,2,1,0:T(8,128)S(1)} %collective-permute-done.low, f32[2,12,8,128]{3,2,1,0:T(8,128)S(1)} %collective-permute-done.1.high, ...), custom_call_target="tpu_custom_call" | custom-call | tf_op jit(solution)/shard_map/slab_pairs/pallas_call | solution.py:243
  47.7 15.2 %tile_pairs.1.own.refs_1_ = f32[4,12,8,128]{3,2,1,0:T(8,128)S(1)} custom-call(f32[4,12,8,128]{3,2,1,0:T(8,128)S(1)} %fusion.37.own.refs_0_.refs_1_, f32[4,12,8,128]{3,2,1,0:T(8,128)S(1)} %fusion.37.own.refs_0_.refs_1_, f32[4,12,8,128]{3,2,1,0:T(8,128)S(1)} %slab_pairs.2.refs_2_, f32[4,12,8,128]{3,2,1,0:T(8,128)S(1)} %collective-permute-done.2.refs_3_, ...), custom_call_target="tpu_custom_call" | custom-call | tf_op jit(solution)/shard_map/tile_pairs/pallas_call | solution.py:243
  62.9 3.3 %collective-permute-start.5 = (f32[2,12,8,128]{3,2,1,0:T(8,128)S(1)}, f32[2,12,8,128]{3,2,1,0:T(8,128)S(1)}, u32[]{:S(2)}, u32[]{:S(2)}) collective-permute-start(f32[2,12,8,128]{3,2,1,0:T(8,128)S(1)} %get-tuple-element.39), channel_id=1, source_target_pairs={{16,0},{32,16},{48,32},{64,48},{80,64},{96,80},{112,96},{17,1},{33... | collective-permute-start | bytes 294920 | tf_op jit(solution)/shard_map/ppermute | solution.py:293
  66.3 4.1 %collective-permute-start.4 = (f32[2,12,8,128]{3,2,1,0:T(8,128)S(1)}, f32[2,12,8,128]{3,2,1,0:T(8,128)S(1)}, u32[]{:S(2)}, u32[]{:S(2)}) collective-permute-start(f32[2,12,8,128]{3,2,1,0:T(8,128)S(1)} %get-tuple-element.40), channel_id=1, source_target_pairs={{0,16},{16,32},{32,48},{48,64},{64,80},{80,96},{96,112},{1,17},{17... | collective-permute-start | bytes 294920 | tf_op jit(solution)/shard_map/ppermute | solution.py:293
  70.3 0.6 collective-permute-done.5.high
  71.0 4.2 %collective-permute-done.4.low = f32[2,12,8,128]{3,2,1,0:T(8,128)S(1)} collective-permute-done((f32[2,12,8,128]{3,2,1,0:T(8,128)S(1)}, f32[2,12,8,128]{3,2,1,0:T(8,128)S(1)}, u32[]{:S(2)}, u32[]{:S(2)}) %collective-permute-start.4) | collective-permute-done | bytes 98336 | tf_op jit(solution)/shard_map/ppermute | solution.py:293
  75.2 1.9 %collective-permute-start.6 = (f32[4,12,8,128]{3,2,1,0:T(8,128)S(1)}, f32[4,12,8,128]{3,2,1,0:T(8,128)S(1)}, u32[]{:S(2)}, u32[]{:S(2)}) collective-permute-start(f32[4,12,8,128]{3,2,1,0:T(8,128)S(1)} %pad_maximum_fusion.2), channel_id=1, source_target_pairs={{0,1},{1,2},{2,3},{3,4},{4,5},{5,6},{6,7},{7,8},{8,9},{9,10},{10,1... | collective-permute-start | bytes 589832 | tf_op jit(solution)/shard_map/ppermute | solution.py:293
  77.2 5.9 %collective-permute-start.7 = (f32[4,12,8,128]{3,2,1,0:T(8,128)S(1)}, f32[4,12,8,128]{3,2,1,0:T(8,128)S(1)}, u32[]{:S(2)}, u32[]{:S(2)}) collective-permute-start(f32[4,12,8,128]{3,2,1,0:T(8,128)S(1)} %pad_maximum_fusion.3), channel_id=1, source_target_pairs={{1,0},{2,1},{3,2},{4,3},{5,4},{6,5},{7,6},{8,7},{9,8},{10,9},{11,1... | collective-permute-start | bytes 589832 | tf_op jit(solution)/shard_map/ppermute | solution.py:293
  83.1 15.2 %near_pairs.3.acc_in = f32[4,12,8,128]{3,2,1,0:T(8,128)S(1)} custom-call(f32[4,12,8,128]{3,2,1,0:T(8,128)S(1)} %tile_pairs.1.own.refs_1_, bf16[256,3072]{1,0:T(8,128)(2,1)S(1)} %fusion.36.select.refs_5_), custom_call_target="tpu_custom_call" | custom-call | tf_op jit(solution)/shard_map/near_pairs/pallas_call | solution.py:243
  98.3 9.3 %slab_pairs.3.refs_2_ = f32[4,12,8,128]{3,2,1,0:T(8,128)S(1)} custom-call(f32[4,12,8,128]{3,2,1,0:T(8,128)S(1)} %tile_pairs.1.own.refs_1_, f32[4,12,8,128]{3,2,1,0:T(8,128)S(1)} %near_pairs.3.acc_in, f32[2,12,8,128]{3,2,1,0:T(8,128)S(1)} %collective-permute-done.4.low, f32[2,12,8,128]{3,2,1,0:T(8,128)S(1)} %collective-permute-done.5.high, ...), custom_call_target="tpu_custom_call" | custom-call | tf_op jit(solution)/shard_map/slab_pairs/pallas_call | solution.py:243
  107.7 15.2 %tile_pairs_final.1 = f32[4,12,8,128]{3,2,1,0:T(8,128)S(1)} custom-call(f32[4,12,8,128]{3,2,1,0:T(8,128)S(1)} %fusion.37.own.refs_0_.refs_1_, f32[4,12,8,128]{3,2,1,0:T(8,128)S(1)} %tile_pairs.1.own.refs_1_, f32[4,12,8,128]{3,2,1,0:T(8,128)S(1)} %slab_pairs.3.refs_2_, f32[4,12,8,128]{3,2,1,0:T(8,128)S(1)} %collective-permute-done.6.refs_3_, ...), custom_call_target="tpu_custom_call" | custom-call | tf_op jit(solution)/shard_map/tile_pairs_final/pallas_call | solution.py:243
  122.9 0.1 reshape.221
  123.0 0.5 copy.30
  123.5 0.7 gather_fusion.1
  124.3 0.1 select_bitcast_fusion
  124.3 1.9 %collective-permute-start.9 = (f32[7,192]{0,1:T(8,128)S(1)}, f32[7,192]{0,1:T(8,128)S(1)}, u32[]{:S(2)}, u32[]{:S(2)}) collective-permute-start(f32[7,192]{0,1:T(8,128)S(1)} %select_bitcast_fusion), channel_id=1, source_target_pairs={{16,0},{32,16},{48,32},{64,48},{80,64},{96,80},{112,96},{17,1},{33... | collective-permute-start | bytes 16136 | tf_op jit(solution)/shard_map/ppermute | solution.py:293
  126.3 0.5 copy.28
  126.8 0.7 gather_fusion
  127.5 0.1 select_bitcast_fusion.1
  127.6 5.4 %collective-permute-start.8 = (f32[7,192]{0,1:T(8,128)S(1)}, f32[7,192]{0,1:T(8,128)S(1)}, u32[]{:S(2)}, u32[]{:S(2)}) collective-permute-start(f32[7,192]{0,1:T(8,128)S(1)} %select_bitcast_fusion.1), channel_id=1, source_target_pairs={{0,16},{16,32},{32,48},{48,64},{64,80},{80,96},{96,112},{1,17},{17... | collective-permute-start | bytes 16136 | tf_op jit(solution)/shard_map/ppermute | solution.py:293
  133.0 0.8 broadcast_select_fusion
  133.8 2.6 %collective-permute-done.8 = f32[7,192]{0,1:T(8,128)S(1)} collective-permute-done((f32[7,192]{0,1:T(8,128)S(1)}, f32[7,192]{0,1:T(8,128)S(1)}, u32[]{:S(2)}, u32[]{:S(2)}) %collective-permute-start.8) | collective-permute-done | bytes 5408 | tf_op jit(solution)/shard_map/ppermute | solution.py:293
  136.6 0.6 pad_maximum_fusion.4
  (56 shorter events, 1.0 us)
Async XLA Ops:
  0.6 11.7 %copy-start = (s32[2,1,2,48]{3,2,1,0:T(2,128)S(1)}, s32[2,1,2,48]{3,2,1,0:T(2,128)}, u32[]{:S(2)}) copy-start(s32[2,1,2,48]{3,2,1,0:T(2,128)} %param.11) | copy-start | bytes 2308
  3.9 26.7 %collective-permute-start = (f32[2,12,8,128]{3,2,1,0:T(8,128)S(1)}, f32[2,12,8,128]{3,2,1,0:T(8,128)S(1)}, u32[]{:S(2)}, u32[]{:S(2)}) collective-permute-start(f32[2,12,8,128]{3,2,1,0:T(8,128)S(1)} %get-tuple-element.46), channel_id=1, source_target_pairs={{0,16},{16,32},{32,48},{48,64},{64,80},{80,96},{96,112},{1,17},{17... | collective-permute-start | bytes 294920 | tf_op jit(solution)/shard_map/ppermute | solution.py:293
  8.1 22.4 %collective-permute-start.1 = (f32[2,12,8,128]{3,2,1,0:T(8,128)S(1)}, f32[2,12,8,128]{3,2,1,0:T(8,128)S(1)}, u32[]{:S(2)}, u32[]{:S(2)}) collective-permute-start(f32[2,12,8,128]{3,2,1,0:T(8,128)S(1)} %get-tuple-element.45), channel_id=1, source_target_pairs={{16,0},{32,16},{48,32},{64,48},{80,64},{96,80},{112,96},{17,1},{33... | collective-permute-start | bytes 294920 | tf_op jit(solution)/shard_map/ppermute | solution.py:293
  30.6 17.1 %collective-permute-start.2 = (f32[4,12,8,128]{3,2,1,0:T(8,128)S(1)}, f32[4,12,8,128]{3,2,1,0:T(8,128)S(1)}, u32[]{:S(2)}, u32[]{:S(2)}) collective-permute-start(f32[4,12,8,128]{3,2,1,0:T(8,128)S(1)} %pad_maximum_fusion), channel_id=1, source_target_pairs={{0,1},{1,2},{2,3},{3,4},{4,5},{5,6},{6,7},{7,8},{8,9},{9,10},{10,1... | collective-permute-start | bytes 589832 | tf_op jit(solution)/shard_map/ppermute | solution.py:293
  32.6 15.1 %collective-permute-start.3 = (f32[4,12,8,128]{3,2,1,0:T(8,128)S(1)}, f32[4,12,8,128]{3,2,1,0:T(8,128)S(1)}, u32[]{:S(2)}, u32[]{:S(2)}) collective-permute-start(f32[4,12,8,128]{3,2,1,0:T(8,128)S(1)} %pad_maximum_fusion.1), channel_id=1, source_target_pairs={{1,0},{2,1},{3,2},{4,3},{5,4},{6,5},{7,6},{8,7},{9,8},{10,9},{11,1... | collective-permute-start | bytes 589832 | tf_op jit(solution)/shard_map/ppermute | solution.py:293
  62.9 8.0 %collective-permute-start.5 = (f32[2,12,8,128]{3,2,1,0:T(8,128)S(1)}, f32[2,12,8,128]{3,2,1,0:T(8,128)S(1)}, u32[]{:S(2)}, u32[]{:S(2)}) collective-permute-start(f32[2,12,8,128]{3,2,1,0:T(8,128)S(1)} %get-tuple-element.39), channel_id=1, source_target_pairs={{16,0},{32,16},{48,32},{64,48},{80,64},{96,80},{112,96},{17,1},{33... | collective-permute-start | bytes 294920 | tf_op jit(solution)/shard_map/ppermute | solution.py:293
  66.3 8.9 %collective-permute-start.4 = (f32[2,12,8,128]{3,2,1,0:T(8,128)S(1)}, f32[2,12,8,128]{3,2,1,0:T(8,128)S(1)}, u32[]{:S(2)}, u32[]{:S(2)}) collective-permute-start(f32[2,12,8,128]{3,2,1,0:T(8,128)S(1)} %get-tuple-element.40), channel_id=1, source_target_pairs={{0,16},{16,32},{32,48},{48,64},{64,80},{80,96},{96,112},{1,17},{17... | collective-permute-start | bytes 294920 | tf_op jit(solution)/shard_map/ppermute | solution.py:293
  75.2 32.4 %collective-permute-start.6 = (f32[4,12,8,128]{3,2,1,0:T(8,128)S(1)}, f32[4,12,8,128]{3,2,1,0:T(8,128)S(1)}, u32[]{:S(2)}, u32[]{:S(2)}) collective-permute-start(f32[4,12,8,128]{3,2,1,0:T(8,128)S(1)} %pad_maximum_fusion.2), channel_id=1, source_target_pairs={{0,1},{1,2},{2,3},{3,4},{4,5},{5,6},{6,7},{7,8},{8,9},{9,10},{10,1... | collective-permute-start | bytes 589832 | tf_op jit(solution)/shard_map/ppermute | solution.py:293
  77.2 30.5 %collective-permute-start.7 = (f32[4,12,8,128]{3,2,1,0:T(8,128)S(1)}, f32[4,12,8,128]{3,2,1,0:T(8,128)S(1)}, u32[]{:S(2)}, u32[]{:S(2)}) collective-permute-start(f32[4,12,8,128]{3,2,1,0:T(8,128)S(1)} %pad_maximum_fusion.3), channel_id=1, source_target_pairs={{1,0},{2,1},{3,2},{4,3},{5,4},{6,5},{7,6},{8,7},{9,8},{10,9},{11,1... | collective-permute-start | bytes 589832 | tf_op jit(solution)/shard_map/ppermute | solution.py:293
  124.3 9.4 %collective-permute-start.9 = (f32[7,192]{0,1:T(8,128)S(1)}, f32[7,192]{0,1:T(8,128)S(1)}, u32[]{:S(2)}, u32[]{:S(2)}) collective-permute-start(f32[7,192]{0,1:T(8,128)S(1)} %select_bitcast_fusion), channel_id=1, source_target_pairs={{16,0},{32,16},{48,32},{64,48},{80,64},{96,80},{112,96},{17,1},{33... | collective-permute-start | bytes 16136 | tf_op jit(solution)/shard_map/ppermute | solution.py:293
  127.6 8.9 %collective-permute-start.8 = (f32[7,192]{0,1:T(8,128)S(1)}, f32[7,192]{0,1:T(8,128)S(1)}, u32[]{:S(2)}, u32[]{:S(2)}) collective-permute-start(f32[7,192]{0,1:T(8,128)S(1)} %select_bitcast_fusion.1), channel_id=1, source_target_pairs={{0,16},{16,32},{32,48},{48,64},{64,80},{80,96},{96,112},{1,17},{17... | collective-permute-start | bytes 16136 | tf_op jit(solution)/shard_map/ppermute | solution.py:293

commit v2 on v1

v2 whole, which is shorter than its diff:
```python
import math

import jax
import jax.numpy as jnp
from jax import lax
from jax.experimental import pallas as pl
from jax.experimental.pallas import tpu as pltpu
from jax.sharding import PartitionSpec as P

SLOTS = 32
LMAX = 4
CZ = 48
BLOCKS = 12

sound_speed = 10.0
smoothing = 0.5
kernel_norm = 21.0 / (16.0 * math.pi * smoothing**3)
grad_scale = -5.0 * kernel_norm / (smoothing * smoothing)
eos_stiff = sound_speed * sound_speed / 7.0
particle_mass = 0.125
viscosity = 0.1
visc_floor = 0.01 * smoothing * smoothing
time_step = 0.01
gravity = 9.81
mass_grad = particle_mass * grad_scale
visc_gain = 2.0 * viscosity * sound_speed * smoothing
FAR = 2.0**50
MIDDLE = 5.5
SPAN = 32 * (BLOCKS + 2)
AROUND = (0, 1, 2, 4, 5, 6, 8, 9, 10)


def pieces(vals):
    top = vals.astype(jnp.bfloat16).astype(jnp.float32)
    rest = vals - top
    second = rest.astype(jnp.bfloat16).astype(jnp.float32)
    return top, second, rest - second


def products(vals):
    both = []
    for prod in (vals * vals, vals * pltpu.roll(vals, 5, 0)):
        rows = [jnp.broadcast_to(prod[k:k + 1], (8, 128)) for k in range(3)]
        both.append(rows[0] + rows[1] + rows[2])
    return both


def neighbour_rows(vals, far_x, far_y, far_z, sub):
    absent = jnp.broadcast_to(vals[6:7], (8, 128)) == 0.0
    shift = jnp.where(sub == 0, far_x, jnp.where(sub == 1, far_y, jnp.where(sub == 2, far_z, 0.0)))
    vals = jnp.where(absent, jnp.where(sub == 0, FAR, 0.0), vals + shift)
    high, mid, low = pieces(vals)
    square, flow = products(vals)
    tail = jnp.ones((8, 128), jnp.float32)
    for k, part in enumerate(pieces(square) + pieces(flow)):
        tail = jnp.where(sub == k, part, tail)
    last = jnp.where(sub == 0, 1.0, 0.0)
    return [high, high, mid, high, low, mid, tail, last]


def column_features(src, far_x, far_y, col, lhs):
    sub = lax.broadcasted_iota(jnp.int32, (8, 128), 0)
    chunk = lax.broadcasted_iota(jnp.int32, (8, 128), 1) // 32
    for beta in range(4):
        rows = []
        for g in range(4):
            if beta < 3:
                vals = src[3 * g + beta]
                level = (chunk + 4 * beta).astype(jnp.float32)
            else:
                none = jnp.zeros((8, 128), jnp.float32)
                below = src[3 * g - 1] if g > 0 else none
                above = src[3 * g + 3] if g < 3 else none
                vals = jnp.where(chunk == 3, below, jnp.where(chunk == 0, above, 0.0))
                level = jnp.where(chunk == 3, -1.0, 12.0)
            rows += neighbour_rows(vals, far_x, far_y, level - MIDDLE, sub)
        for h in range(2):
            flat = jnp.concatenate(rows[16 * h:16 * h + 16], axis=0).T.astype(jnp.bfloat16)
            lanes = slice(128 * h, 128 * h + 128)
            if beta < 3:
                lhs[col, 128 * beta + 32:128 * beta + 160, lanes] = flat
            else:
                lhs[col, 0:32, lanes] = flat[96:128]
                lhs[col, 416:448, lanes] = flat[0:32]


def spread_positions(count, lhs, select, tiles):
    k = lax.broadcasted_iota(jnp.int32, (256, 384), 0)
    n = lax.broadcasted_iota(jnp.int32, (256, 384), 1)
    part = k % 64
    hit = (part % 8 == n // 128) & ((part // 8) % 2 == 0) & (part < 40) & (k // 64 == (n % 128) // 32)
    select[...] = jnp.where(hit, 1.0, 0.0).astype(jnp.bfloat16)

    def four(n, _):
        rows = lhs[pl.ds(4 * n, 4)].reshape(4 * SPAN, 256)
        out = jnp.dot(rows, select[...], preferred_element_type=jnp.float32)
        for c in range(4):
            for f in range(3):
                part = out[SPAN * c:SPAN * (c + 1), 128 * f:128 * f + 128]
                tiles[4 * n + c, f] = part.reshape(SPAN // 8, 8, 128)
        return 0
    lax.fori_loop(0, count // 4, four, 0)


def swap_chunks(load, store):
    chunk = lax.broadcasted_iota(jnp.int32, (8, 128), 1) // 32
    for beta in range(3):
        rows = [load(3 * g + beta) for g in range(4)]
        for q in range(4):
            res = rows[q]
            for g in range(4):
                if g != q:
                    res = jnp.where(chunk == g, pltpu.roll(rows[g], (32 * (g - q)) % 128, 1), res)
            store(4 * beta + q, res)


def swap_back(load, store):
    chunk = lax.broadcasted_iota(jnp.int32, (8, 128), 1) // 32
    for beta in range(3):
        rows = [load(4 * beta + q) for q in range(4)]
        for g in range(4):
            res = rows[g]
            for q in range(4):
                if g != q:
                    res = jnp.where(chunk == q, pltpu.roll(rows[q], (32 * (q - g)) % 128, 1), res)
            store(3 * g + beta, res)


def chunk_masks():
    chunk = lax.broadcasted_iota(jnp.int32, (16, 128), 1) // 32
    return [jnp.where(chunk == g, 1.0, 0.0).astype(jnp.bfloat16) for g in range(4)]


def fill_weights(weights):
    sub = lax.broadcasted_iota(jnp.int32, (8, 128), 0)
    zero = jnp.zeros((8, 128), jnp.float32)
    for n, k in ((2, 6), (3, 7)):
        one = jnp.where(sub == k, 1.0, 0.0)
        part = jnp.concatenate([one, zero], axis=0).astype(jnp.bfloat16)
        for g, mask in enumerate(chunk_masks()):
            for p in range(3):
                row = 64 * g + 16 * p
                weights[row:row + 16, 128 * n:128 * n + 128] = part * mask


def center_weights(rows, weights):
    sub = lax.broadcasted_iota(jnp.int32, (8, 128), 0)
    parts = pieces(rows)
    square, flow = products(rows)
    place = [jnp.where(sub < 3, -2.0 * p, 0.0) for p in parts]
    speed = [jnp.where(sub < 3, pltpu.roll(p, 5, 0), jnp.where(sub < 6, pltpu.roll(p, 3, 0), 0.0))
             for p in parts]

    def tail(lead, const):
        top, second, third = const
        return [jnp.where(sub == 6, top, jnp.where(sub == 7, second, lead)),
                jnp.where(sub == 0, third, 0.0)]

    def over(k):
        return [jnp.broadcast_to(p[k:k + 1], (8, 128)) for p in parts]
    masks = chunk_masks()
    tails = [tail(jnp.where(sub < 3, 1.0, 0.0), pieces(square)),
             tail(jnp.where((sub >= 3) & (sub < 6), -1.0, 0.0), pieces(-flow)),
             tail(jnp.zeros((8, 128), jnp.float32), over(6)),
             tail(jnp.zeros((8, 128), jnp.float32), over(7))]
    for n, last in enumerate(tails):
        blocks = [(3, last)]
        if n < 2:
            p = (place, speed)[n]
            blocks += [(0, p[:2]), (1, [p[0], p[2]]), (2, p[:2])]
        for at, part in blocks:
            part = jnp.concatenate(part, axis=0).astype(jnp.bfloat16)
            for g, mask in enumerate(masks):
                row = 64 * g + 16 * at
                weights[row:row + 16, 128 * n:128 * n + 128] = part * mask


def pair(acc, terms, tile):
    r2, approach, dens, ratio = terms
    r2 = jnp.maximum(r2, 1e-30)
    support = jnp.maximum(1.0 - r2 * lax.rsqrt(r2), 0.0)
    slope = support * support * support
    visc = jnp.maximum(approach, 0.0) / ((r2 + visc_floor) * dens)
    force = (ratio + visc) * slope
    return (acc[0] + force * tile[0], acc[1] + force * tile[1], acc[2] + force * tile[2],
            acc[3] + slope * approach, acc[4] + force)


def center_blocks(own, blocks):
    sub = lax.broadcasted_iota(jnp.int32, (8, 128), 0)

    def one(c, _):
        far_x = (c // 2).astype(jnp.float32) - 0.5
        far_y = (c % 2).astype(jnp.float32) - 0.5

        def store(r, vals):
            shift = jnp.where(sub == 0, far_x, jnp.where(sub == 1, far_y,
                              jnp.where(sub == 2, r - MIDDLE, 0.0)))
            blocks[c, r] = vals + shift
        swap_chunks(lambda r: own[c, r], store)
        return 0
    lax.fori_loop(0, 4, one, 0)


def all_pairs(blocks, lhs, tiles, bufs, emit):
    def first_column(c):
        return 4 * (c // 2) + c % 2

    def produce(n, weights, result):
        n = jnp.minimum(n, 4 * BLOCKS - 1)
        c, b = n // BLOCKS, n % BLOCKS
        center_weights(blocks[c, b], weights)
        rows = pl.ds(pl.multiple_of(32 * b, 32), 96)
        near = jnp.concatenate([lhs[first_column(c) + j, rows, :] for j in AROUND], axis=0)
        result[...] = jnp.dot(near, weights[...], preferred_element_type=jnp.float32)

    def consume(n, result):
        c, b = n // BLOCKS, n % BLOCKS
        acc = tuple(jnp.zeros((8, 128), jnp.float32) for _ in range(5))
        for k, j in enumerate(AROUND):
            for i in range(12):
                r = 96 * k + 8 * i
                terms = [result[r:r + 8, 128 * n:128 * n + 128] for n in range(4)]
                acc = pair(acc, terms, [tiles[first_column(c) + j, f, 4 * b + i] for f in range(3)])
        sums = [jnp.sum(a, axis=0, keepdims=True) for a in acc]
        rows = blocks[c, b]
        sums = [rows[k:k + 1] * sums[4] - sums[k] for k in range(3)] + sums[3:4]
        emit(c, b, jnp.concatenate(sums + [jnp.zeros((4, 128), jnp.float32)], axis=0))

    w0, r0, w1, r1 = bufs
    fill_weights(w0)
    fill_weights(w1)
    produce(0, w0, r0)

    def step(m, _):
        produce(2 * m + 1, w1, r1)
        consume(2 * m, r0)
        produce(2 * m + 2, w0, r0)
        consume(2 * m + 1, r1)
        return 0
    lax.fori_loop(0, 2 * BLOCKS, step, 0)


def pass_kernel(final, base, own, low, high, front, back, out,
                cols, blocks, lhs, tiles, select, res, *bufs):
    center_blocks(own, blocks)
    for i in range(2):
        for y in range(2):
            cols[4 * (i + 1) + y + 1] = own[2 * i + y]
        cols[1 + i] = low[i]
        cols[13 + i] = high[i]
    for i in range(4):
        cols[4 * i] = front[i]
        cols[4 * i + 3] = back[i]

    def one(j, _):
        column_features(cols.at[j], (j // 4).astype(jnp.float32) - 1.5,
                        (j % 4).astype(jnp.float32) - 1.5, j, lhs)
        return 0
    lax.fori_loop(0, 16, one, 0)
    spread_positions(16, lhs, select, tiles)

    def emit(c, b, sums):
        res[c, b] = sums
    all_pairs(blocks, lhs, tiles, bufs, emit)

    def finish(c, _):
        def store(r, rates):
            now = base[c, r]
            present = now[6:7] != 0.0
            ax = -mass_grad * rates[0:1]
            ay = -mass_grad * rates[1:2]
            az = -mass_grad * rates[2:3] - gravity
            drift = -mass_grad * rates[3:4]
            half = 0.5 * time_step
            if not final:
                dens = now[6:7] + half * drift
                dens = jnp.where(present, dens, 1.0)
                ratio = eos_stiff * (dens**7 - 1.0) / (dens * dens)
                vals = [now[0:1] + half * now[3:4], now[1:2] + half * now[4:5],
                        now[2:3] + half * now[5:6], now[3:4] + half * ax,
                        now[4:5] + half * ay, now[5:6] + half * az, dens, ratio]
            else:
                v1 = [now[3:4] + time_step * ax, now[4:5] + time_step * ay,
                      now[5:6] + time_step * az]
                vals = [now[k:k + 1] + half * (now[3 + k:4 + k] + v1[k]) for k in range(3)]
                vals += v1 + [now[6:7] + time_step * drift, now[7:8]]
            full = jnp.concatenate(vals, axis=0)
            out[c, r] = jnp.where(jnp.broadcast_to(present, (8, 128)), full, 0.0)
        swap_back(lambda r: res[c, r], store)
        return 0
    lax.fori_loop(0, 4, finish, 0)


def rates_pass(final, base, own):
    low = shifted(own[2:4], "slab", 1)
    high = shifted(own[0:2], "slab", -1)
    front = shifted(jnp.concatenate([low[1:2], own[1:2], own[3:4], high[1:2]]), "tile", 1)
    back = shifted(jnp.concatenate([low[0:1], own[0:1], own[2:3], high[0:1]]), "tile", -1)

    def body(*refs):
        pass_kernel(final, *refs)
    work = [pltpu.VMEM((256, 512), jnp.bfloat16), pltpu.VMEM((864, 512), jnp.float32)]
    return pl.pallas_call(
        body,
        out_shape=jax.ShapeDtypeStruct((4, BLOCKS, 8, 128), jnp.float32),
        scratch_shapes=[pltpu.VMEM((16, BLOCKS, 8, 128), jnp.float32),
                        pltpu.VMEM((4, BLOCKS, 8, 128), jnp.float32),
                        pltpu.VMEM((16, SPAN, 256), jnp.bfloat16),
                        pltpu.VMEM((16, 3, SPAN // 8, 8, 128), jnp.float32),
                        pltpu.VMEM((256, 384), jnp.bfloat16),
                        pltpu.VMEM((4, BLOCKS, 8, 128), jnp.float32),
                        *work, *work],
        compiler_params=pltpu.CompilerParams(vmem_limit_bytes=40 << 20),
        name="correct_pass" if final else "predict_pass",
    )(base, own, low, high, front, back)


def slot_mask(cell_counts):
    slot = lax.broadcasted_iota(jnp.int32, cell_counts.shape + (SLOTS,), cell_counts.ndim)
    return slot < cell_counts[..., None]


def pack_leavers(face_state, face_count, face_leave):
    cell_total = face_count.shape[0] * face_count.shape[1]
    row_total = cell_total * LMAX // 2
    leave_quota = face_leave.reshape(cell_total)
    occupancy = face_count.reshape(cell_total)
    row_ends = jnp.cumsum(leave_quota, dtype=jnp.int32)
    starts = row_ends - leave_quota
    row_ids = jnp.arange(row_total, dtype=jnp.int32)
    owner_mask = (starts[None, :] <= row_ids[:, None]) & (row_ends[None, :] > row_ids[:, None])
    root = jnp.arange(cell_total, dtype=jnp.int32) * SLOTS + occupancy - leave_quota - starts
    source_row = jnp.sum(jnp.where(owner_mask, root[None, :], 0), axis=1, dtype=jnp.int32) + row_ids
    flat_face = face_state.reshape(7, cell_total * SLOTS)
    return jnp.take(flat_face, source_row, axis=1)


def shifted(value, axis, steps):
    count = lax.axis_size(axis)
    leading, last = (max(0, -steps), min(count, count - steps))
    return lax.ppermute(value, axis, [(source, source + steps) for source in range(leading, last)])


def start_fields(particles, counts):
    mask = slot_mask(counts).reshape(2, 2, CZ * SLOTS)
    dens = jnp.where(mask, particles[6], 1.0)
    ratio = eos_stiff * (dens**7 - 1.0) / (dens * dens)
    fields = jnp.concatenate([particles, ratio[None]], axis=0)
    fields = jnp.where(mask[None], fields, 0.0)
    return fields.reshape(8, 4, BLOCKS, 128).transpose(1, 2, 0, 3)


def finish_fields(updated):
    return updated.transpose(2, 0, 1, 3)[:7].reshape(7, 2, 2, CZ * SLOTS)


def shards(particles, counts, leavers):
    fields = start_fields(particles, counts)
    middle = rates_pass(False, fields, fields)
    updated = finish_fields(rates_pass(True, fields, middle))
    remain = counts.at[0].add(-leavers[0, 0]).at[1].add(-leavers[1, 0])
    kept = jnp.where(slot_mask(remain).reshape(1, 2, 2, CZ * SLOTS), updated, 0.0)
    lower_rows = pack_leavers(updated[:, 0], counts[0], leavers[0, 0])
    upper_rows = pack_leavers(updated[:, 1], counts[1], leavers[1, 0])
    from_below = shifted(upper_rows, "slab", 1)
    from_above = shifted(lower_rows, "slab", -1)
    return (kept, jnp.stack([from_below, from_above], axis=0))


def solution(mesh):
    return jax.shard_map(
        shards,
        mesh=mesh,
        in_specs=(
            P(None, "slab", "tile", None),
            P("slab", "tile", None),
            P(None, "slab", "tile", None),
        ),
        out_specs=(P(None, "slab", "tile", None), P(None, None, ("slab", "tile"))),
        check_vma=False,
    )
```

time: 139 us -> 127 us (0.914)
  Pallas kernels: 79.5 us -> 59.7 us
  waiting for transfers between devices: 7.49 us -> 18 us
  other arithmetic: 4.71 us -> 3.31 us
    pallas_call x6 -> x2, Pallas kernels: 79.5 us -> 59.7 us  [rates_pass(): pl.pallas_call(body, out_shape=jax.ShapeDtypeStruct((4, BLOCKS, 8, 128),...]
    ppermute x10, waiting for transfers between devices: 7.49 us -> 18 us  [shifted(): lax.ppermute(value, axis, [(source, source + steps) for source in range(l...]
  transfers between devices with their start and end apart: 10 -> 10, of which waited for: 3 -> 8; matrix products, arithmetic and copies ran while one was open for 4% -> 3% of each run, Pallas kernels for 36% -> 0%
where the time goes in v2:
time: 127 us; the launch traced here: 126 us
  Pallas kernels  59.7 us (47%)
  starting transfers between devices  38.3 us (30%)
  waiting for transfers between devices  18 us (14%)
  local copies, waits for them, and re-layouts  5.85 us (5%)
  other arithmetic  3.31 us (3%)
    pallas_call x2, Pallas kernels, rates_pass(): pl.pallas_call(body, out_shape=jax.ShapeDtypeStruct((4, BLOCKS, 8, 128),...  59.7 us
    ppermute x10, starting transfers between devices, shifted(): lax.ppermute(value, axis, [(source, source + steps) for source in range(l...  38.3 us
    ppermute x10, waiting for transfers between devices, shifted(): lax.ppermute(value, axis, [(source, source + steps) for source in range(l...  18 us
  transfers between devices with their start and end apart: 10, of which 8 were waited for; matrix products, arithmetic and copies ran while one was open for 3% of the time, Pallas kernels for 0%

profile of v2, /device:TPU:10, one launch (start us, length us, event | category | flops | bytes accessed | tf_op | source)
XLA Modules:
  0.0 126.2 jit_solution(2361047532015525205)
XLA Ops:
  0.6 0.7 copy.36
  1.4 0.1 lt.50
  1.5 0.1 lt.48
  1.7 1.1 concatenate.24
  2.8 0.8 multiply_divide_fusion
  3.6 0.1 copy.25
  3.9 4.2 %collective-permute-start = (f32[2,12,8,128]{3,2,1,0:T(8,128)S(1)}, f32[2,12,8,128]{3,2,1,0:T(8,128)S(1)}, u32[]{:S(2)}, u32[]{:S(2)}) collective-permute-start(f32[2,12,8,128]{3,2,1,0:T(8,128)S(1)} %get-tuple-element.46), channel_id=1, source_target_pairs={{0,16},{16,32},{32,48},{48,64},{64,80},{80,96},{96,112},{1,17},{17... | collective-permute-start | bytes 294920 | tf_op jit(solution)/shard_map/ppermute | solution.py:342
  8.1 4.0 %collective-permute-start.1 = (f32[2,12,8,128]{3,2,1,0:T(8,128)S(1)}, f32[2,12,8,128]{3,2,1,0:T(8,128)S(1)}, u32[]{:S(2)}, u32[]{:S(2)}) collective-permute-start(f32[2,12,8,128]{3,2,1,0:T(8,128)S(1)} %get-tuple-element.45), channel_id=1, source_target_pairs={{16,0},{32,16},{48,32},{64,48},{80,64},{96,80},{112,96},{17,1},{33... | collective-permute-start | bytes 294920 | tf_op jit(solution)/shard_map/ppermute | solution.py:342
  12.2 0.1 reshape_squeeze.22
  12.3 0.1 reshape.249
  12.4 0.1 reshape_squeeze.19
  12.5 0.1 reshape.248
  12.6 0.1 lt.44
  12.7 0.1 lt.45
  12.9 0.1 reshape_squeeze.23
  13.0 0.1 reduce-window.15
  13.1 0.1 reduce.5
  13.2 0.1 select_reduce_fusion
  13.4 0.1 reduce-window.14
  13.6 0.1 reduce.4
  13.7 0.1 select_reduce_fusion.1
  13.9 2.3 %collective-permute-done.1.refs_3_ = f32[2,12,8,128]{3,2,1,0:T(8,128)S(1)} collective-permute-done((f32[2,12,8,128]{3,2,1,0:T(8,128)S(1)}, f32[2,12,8,128]{3,2,1,0:T(8,128)S(1)}, u32[]{:S(2)}, u32[]{:S(2)}) %collective-permute-start.1) | collective-permute-done | bytes 98336 | tf_op jit(solution)/shard_map/ppermute | solution.py:342
  16.2 1.9 %collective-permute-start.2 = (f32[4,12,8,128]{3,2,1,0:T(8,128)S(1)}, f32[4,12,8,128]{3,2,1,0:T(8,128)S(1)}, u32[]{:S(2)}, u32[]{:S(2)}) collective-permute-start(f32[4,12,8,128]{3,2,1,0:T(8,128)S(1)} %pad_maximum_fusion), channel_id=1, source_target_pairs={{0,1},{1,2},{2,3},{3,4},{4,5},{5,6},{6,7},{7,8},{8,9},{9,10},{10,1... | collective-permute-start | bytes 589832 | tf_op jit(solution)/shard_map/ppermute | solution.py:342
  18.1 5.8 %collective-permute-start.3 = (f32[4,12,8,128]{3,2,1,0:T(8,128)S(1)}, f32[4,12,8,128]{3,2,1,0:T(8,128)S(1)}, u32[]{:S(2)}, u32[]{:S(2)}) collective-permute-start(f32[4,12,8,128]{3,2,1,0:T(8,128)S(1)} %pad_maximum_fusion.1), channel_id=1, source_target_pairs={{1,0},{2,1},{3,2},{4,3},{5,4},{6,5},{7,6},{8,7},{9,8},{10,9},{11,1... | collective-permute-start | bytes 589832 | tf_op jit(solution)/shard_map/ppermute | solution.py:342
  23.9 1.4 %collective-permute-done.2.refs_4_ = f32[4,12,8,128]{3,2,1,0:T(8,128)S(1)} collective-permute-done((f32[4,12,8,128]{3,2,1,0:T(8,128)S(1)}, f32[4,12,8,128]{3,2,1,0:T(8,128)S(1)}, u32[]{:S(2)}, u32[]{:S(2)}) %collective-permute-start.2) | collective-permute-done | bytes 196640 | tf_op jit(solution)/shard_map/ppermute | solution.py:342
  25.3 1.8 %collective-permute-done.3.refs_5_ = f32[4,12,8,128]{3,2,1,0:T(8,128)S(1)} collective-permute-done((f32[4,12,8,128]{3,2,1,0:T(8,128)S(1)}, f32[4,12,8,128]{3,2,1,0:T(8,128)S(1)}, u32[]{:S(2)}, u32[]{:S(2)}) %collective-permute-start.3) | collective-permute-done | bytes 196640 | tf_op jit(solution)/shard_map/ppermute | solution.py:342
  27.1 29.8 %predict_pass.1.refs_1_ = f32[4,12,8,128]{3,2,1,0:T(8,128)S(1)} custom-call(f32[4,12,8,128]{3,2,1,0:T(8,128)S(1)} %fusion.refs_0_.refs_1_, f32[4,12,8,128]{3,2,1,0:T(8,128)S(1)} %fusion.refs_0_.refs_1_, f32[2,12,8,128]{3,2,1,0:T(8,128)S(1)} %collective-permute-done.refs_2_, f32[2,12,8,128]{3,2,1,0:T(8,128)S(1)} %collective-permute-done.1.refs_3_, ...), custom_call_target="tpu_custom_call" | custom-call | tf_op jit(solution)/shard_map/predict_pass/pallas_call | solution.py:304
  56.9 5.0 %collective-permute-start.5 = (f32[2,12,8,128]{3,2,1,0:T(8,128)S(1)}, f32[2,12,8,128]{3,2,1,0:T(8,128)S(1)}, u32[]{:S(2)}, u32[]{:S(2)}) collective-permute-start(f32[2,12,8,128]{3,2,1,0:T(8,128)S(1)} %get-tuple-element.39), channel_id=1, source_target_pairs={{16,0},{32,16},{48,32},{64,48},{80,64},{96,80},{112,96},{17,1},{33... | collective-permute-start | bytes 294920 | tf_op jit(solution)/shard_map/ppermute | solution.py:342
  61.9 2.4 %collective-permute-start.4 = (f32[2,12,8,128]{3,2,1,0:T(8,128)S(1)}, f32[2,12,8,128]{3,2,1,0:T(8,128)S(1)}, u32[]{:S(2)}, u32[]{:S(2)}) collective-permute-start(f32[2,12,8,128]{3,2,1,0:T(8,128)S(1)} %get-tuple-element.40), channel_id=1, source_target_pairs={{0,16},{16,32},{32,48},{48,64},{64,80},{80,96},{96,112},{1,17},{17... | collective-permute-start | bytes 294920 | tf_op jit(solution)/shard_map/ppermute | solution.py:342
  64.3 0.8 collective-permute-done.5.refs_3_
  65.1 5.7 %collective-permute-done.4.refs_2_ = f32[2,12,8,128]{3,2,1,0:T(8,128)S(1)} collective-permute-done((f32[2,12,8,128]{3,2,1,0:T(8,128)S(1)}, f32[2,12,8,128]{3,2,1,0:T(8,128)S(1)}, u32[]{:S(2)}, u32[]{:S(2)}) %collective-permute-start.4) | collective-permute-done | bytes 98336 | tf_op jit(solution)/shard_map/ppermute | solution.py:342
  70.9 1.9 %collective-permute-start.6 = (f32[4,12,8,128]{3,2,1,0:T(8,128)S(1)}, f32[4,12,8,128]{3,2,1,0:T(8,128)S(1)}, u32[]{:S(2)}, u32[]{:S(2)}) collective-permute-start(f32[4,12,8,128]{3,2,1,0:T(8,128)S(1)} %pad_maximum_fusion.2), channel_id=1, source_target_pairs={{0,1},{1,2},{2,3},{3,4},{4,5},{5,6},{6,7},{7,8},{8,9},{9,10},{10,1... | collective-permute-start | bytes 589832 | tf_op jit(solution)/shard_map/ppermute | solution.py:342
  72.8 5.8 %collective-permute-start.7 = (f32[4,12,8,128]{3,2,1,0:T(8,128)S(1)}, f32[4,12,8,128]{3,2,1,0:T(8,128)S(1)}, u32[]{:S(2)}, u32[]{:S(2)}) collective-permute-start(f32[4,12,8,128]{3,2,1,0:T(8,128)S(1)} %pad_maximum_fusion.3), channel_id=1, source_target_pairs={{1,0},{2,1},{3,2},{4,3},{5,4},{6,5},{7,6},{8,7},{9,8},{10,9},{11,1... | collective-permute-start | bytes 589832 | tf_op jit(solution)/shard_map/ppermute | solution.py:342
  78.6 1.4 %collective-permute-done.6.refs_4_ = f32[4,12,8,128]{3,2,1,0:T(8,128)S(1)} collective-permute-done((f32[4,12,8,128]{3,2,1,0:T(8,128)S(1)}, f32[4,12,8,128]{3,2,1,0:T(8,128)S(1)}, u32[]{:S(2)}, u32[]{:S(2)}) %collective-permute-start.6) | collective-permute-done | bytes 196640 | tf_op jit(solution)/shard_map/ppermute | solution.py:342
  80.0 1.8 %collective-permute-done.7.refs_5_ = f32[4,12,8,128]{3,2,1,0:T(8,128)S(1)} collective-permute-done((f32[4,12,8,128]{3,2,1,0:T(8,128)S(1)}, f32[4,12,8,128]{3,2,1,0:T(8,128)S(1)}, u32[]{:S(2)}, u32[]{:S(2)}) %collective-permute-start.7) | collective-permute-done | bytes 196640 | tf_op jit(solution)/shard_map/ppermute | solution.py:342
  81.8 29.8 %correct_pass.1 = f32[4,12,8,128]{3,2,1,0:T(8,128)S(1)} custom-call(f32[4,12,8,128]{3,2,1,0:T(8,128)S(1)} %fusion.refs_0_.refs_1_, f32[4,12,8,128]{3,2,1,0:T(8,128)S(1)} %predict_pass.1.refs_1_, f32[2,12,8,128]{3,2,1,0:T(8,128)S(1)} %collective-permute-done.4.refs_2_, f32[2,12,8,128]{3,2,1,0:T(8,128)S(1)} %collective-permute-done.5.refs_3_, ...), custom_call_target="tpu_custom_call" | custom-call | tf_op jit(solution)/shard_map/correct_pass/pallas_call | solution.py:304
  111.6 0.1 reshape.221
  111.8 0.5 copy.30
  112.3 0.7 gather_fusion.1
  113.0 0.1 select_bitcast_fusion
  113.1 2.2 %collective-permute-start.9 = (f32[7,192]{0,1:T(8,128)S(1)}, f32[7,192]{0,1:T(8,128)S(1)}, u32[]{:S(2)}, u32[]{:S(2)}) collective-permute-start(f32[7,192]{0,1:T(8,128)S(1)} %select_bitcast_fusion), channel_id=1, source_target_pairs={{16,0},{32,16},{48,32},{64,48},{80,64},{96,80},{112,96},{17,1},{33... | collective-permute-start | bytes 16136 | tf_op jit(solution)/shard_map/ppermute | solution.py:342
  115.3 0.5 copy.28
  115.8 0.7 gather_fusion
  116.5 0.1 select_bitcast_fusion.1
  116.6 5.2 %collective-permute-start.8 = (f32[7,192]{0,1:T(8,128)S(1)}, f32[7,192]{0,1:T(8,128)S(1)}, u32[]{:S(2)}, u32[]{:S(2)}) collective-permute-start(f32[7,192]{0,1:T(8,128)S(1)} %select_bitcast_fusion.1), channel_id=1, source_target_pairs={{0,16},{16,32},{32,48},{48,64},{64,80},{80,96},{96,112},{1,17},{17... | collective-permute-start | bytes 16136 | tf_op jit(solution)/shard_map/ppermute | solution.py:342
  121.7 0.8 broadcast_select_fusion
  122.6 2.9 %collective-permute-done.8 = f32[7,192]{0,1:T(8,128)S(1)} collective-permute-done((f32[7,192]{0,1:T(8,128)S(1)}, f32[7,192]{0,1:T(8,128)S(1)}, u32[]{:S(2)}, u32[]{:S(2)}) %collective-permute-start.8) | collective-permute-done | bytes 5408 | tf_op jit(solution)/shard_map/ppermute | solution.py:342
  125.6 0.6 pad_maximum_fusion.4
  (41 shorter events, 0.9 us)
Async XLA Ops:
  0.6 11.6 %copy-start = (s32[2,1,2,48]{3,2,1,0:T(2,128)S(1)}, s32[2,1,2,48]{3,2,1,0:T(2,128)}, u32[]{:S(2)}) copy-start(s32[2,1,2,48]{3,2,1,0:T(2,128)} %param.11) | copy-start | bytes 2308
  3.9 12.2 %collective-permute-start = (f32[2,12,8,128]{3,2,1,0:T(8,128)S(1)}, f32[2,12,8,128]{3,2,1,0:T(8,128)S(1)}, u32[]{:S(2)}, u32[]{:S(2)}) collective-permute-start(f32[2,12,8,128]{3,2,1,0:T(8,128)S(1)} %get-tuple-element.46), channel_id=1, source_target_pairs={{0,16},{16,32},{32,48},{48,64},{64,80},{80,96},{96,112},{1,17},{17... | collective-permute-start | bytes 294920 | tf_op jit(solution)/shard_map/ppermute | solution.py:342
  8.1 8.0 %collective-permute-start.1 = (f32[2,12,8,128]{3,2,1,0:T(8,128)S(1)}, f32[2,12,8,128]{3,2,1,0:T(8,128)S(1)}, u32[]{:S(2)}, u32[]{:S(2)}) collective-permute-start(f32[2,12,8,128]{3,2,1,0:T(8,128)S(1)} %get-tuple-element.45), channel_id=1, source_target_pairs={{16,0},{32,16},{48,32},{64,48},{80,64},{96,80},{112,96},{17,1},{33... | collective-permute-start | bytes 294920 | tf_op jit(solution)/shard_map/ppermute | solution.py:342
  16.2 9.1 %collective-permute-start.2 = (f32[4,12,8,128]{3,2,1,0:T(8,128)S(1)}, f32[4,12,8,128]{3,2,1,0:T(8,128)S(1)}, u32[]{:S(2)}, u32[]{:S(2)}) collective-permute-start(f32[4,12,8,128]{3,2,1,0:T(8,128)S(1)} %pad_maximum_fusion), channel_id=1, source_target_pairs={{0,1},{1,2},{2,3},{3,4},{4,5},{5,6},{6,7},{7,8},{8,9},{9,10},{10,1... | collective-permute-start | bytes 589832 | tf_op jit(solution)/shard_map/ppermute | solution.py:342
  18.1 8.9 %collective-permute-start.3 = (f32[4,12,8,128]{3,2,1,0:T(8,128)S(1)}, f32[4,12,8,128]{3,2,1,0:T(8,128)S(1)}, u32[]{:S(2)}, u32[]{:S(2)}) collective-permute-start(f32[4,12,8,128]{3,2,1,0:T(8,128)S(1)} %pad_maximum_fusion.1), channel_id=1, source_target_pairs={{1,0},{2,1},{3,2},{4,3},{5,4},{6,5},{7,6},{8,7},{9,8},{10,9},{11,1... | collective-permute-start | bytes 589832 | tf_op jit(solution)/shard_map/ppermute | solution.py:342
  56.9 8.2 %collective-permute-start.5 = (f32[2,12,8,128]{3,2,1,0:T(8,128)S(1)}, f32[2,12,8,128]{3,2,1,0:T(8,128)S(1)}, u32[]{:S(2)}, u32[]{:S(2)}) collective-permute-start(f32[2,12,8,128]{3,2,1,0:T(8,128)S(1)} %get-tuple-element.39), channel_id=1, source_target_pairs={{16,0},{32,16},{48,32},{64,48},{80,64},{96,80},{112,96},{17,1},{33... | collective-permute-start | bytes 294920 | tf_op jit(solution)/shard_map/ppermute | solution.py:342
  61.9 8.9 %collective-permute-start.4 = (f32[2,12,8,128]{3,2,1,0:T(8,128)S(1)}, f32[2,12,8,128]{3,2,1,0:T(8,128)S(1)}, u32[]{:S(2)}, u32[]{:S(2)}) collective-permute-start(f32[2,12,8,128]{3,2,1,0:T(8,128)S(1)} %get-tuple-element.40), channel_id=1, source_target_pairs={{0,16},{16,32},{32,48},{48,64},{64,80},{80,96},{96,112},{1,17},{17... | collective-permute-start | bytes 294920 | tf_op jit(solution)/shard_map/ppermute | solution.py:342
  70.9 9.1 %collective-permute-start.6 = (f32[4,12,8,128]{3,2,1,0:T(8,128)S(1)}, f32[4,12,8,128]{3,2,1,0:T(8,128)S(1)}, u32[]{:S(2)}, u32[]{:S(2)}) collective-permute-start(f32[4,12,8,128]{3,2,1,0:T(8,128)S(1)} %pad_maximum_fusion.2), channel_id=1, source_target_pairs={{0,1},{1,2},{2,3},{3,4},{4,5},{5,6},{6,7},{7,8},{8,9},{9,10},{10,1... | collective-permute-start | bytes 589832 | tf_op jit(solution)/shard_map/ppermute | solution.py:342
  72.8 8.9 %collective-permute-start.7 = (f32[4,12,8,128]{3,2,1,0:T(8,128)S(1)}, f32[4,12,8,128]{3,2,1,0:T(8,128)S(1)}, u32[]{:S(2)}, u32[]{:S(2)}) collective-permute-start(f32[4,12,8,128]{3,2,1,0:T(8,128)S(1)} %pad_maximum_fusion.3), channel_id=1, source_target_pairs={{1,0},{2,1},{3,2},{4,3},{5,4},{6,5},{7,6},{8,7},{9,8},{10,9},{11,1... | collective-permute-start | bytes 589832 | tf_op jit(solution)/shard_map/ppermute | solution.py:342
  113.1 9.4 %collective-permute-start.9 = (f32[7,192]{0,1:T(8,128)S(1)}, f32[7,192]{0,1:T(8,128)S(1)}, u32[]{:S(2)}, u32[]{:S(2)}) collective-permute-start(f32[7,192]{0,1:T(8,128)S(1)} %select_bitcast_fusion), channel_id=1, source_target_pairs={{16,0},{32,16},{48,32},{64,48},{80,64},{96,80},{112,96},{17,1},{33... | collective-permute-start | bytes 16136 | tf_op jit(solution)/shard_map/ppermute | solution.py:342
  116.6 8.9 %collective-permute-start.8 = (f32[7,192]{0,1:T(8,128)S(1)}, f32[7,192]{0,1:T(8,128)S(1)}, u32[]{:S(2)}, u32[]{:S(2)}) collective-permute-start(f32[7,192]{0,1:T(8,128)S(1)} %select_bitcast_fusion.1), channel_id=1, source_target_pairs={{0,16},{16,32},{32,48},{48,64},{64,80},{80,96},{96,112},{1,17},{17... | collective-permute-start | bytes 16136 | tf_op jit(solution)/shard_map/ppermute | solution.py:342

commit v3 on v2

--- a/solution.py
+++ b/solution.py
@@ -227,31 +227,35 @@
         sums = [rows[k:k + 1] * sums[4] - sums[k] for k in range(3)] + sums[3:4]
         emit(c, b, jnp.concatenate(sums + [jnp.zeros((4, 128), jnp.float32)], axis=0))
 
-    w0, r0, w1, r1 = bufs
-    fill_weights(w0)
-    fill_weights(w1)
-    produce(0, w0, r0)
+    fill_weights(bufs[0])
+    fill_weights(bufs[2])
+    produce(0, *bufs[:2])
 
     def step(m, _):
-        produce(2 * m + 1, w1, r1)
-        consume(2 * m, r0)
-        produce(2 * m + 2, w0, r0)
-        consume(2 * m + 1, r1)
-        return 0
-    lax.fori_loop(0, 2 * BLOCKS, step, 0)
-
-
-def pass_kernel(final, base, own, low, high, front, back, out,
+        for k in range(4):
+            consume(4 * m + k, bufs[2 * (k % 2) + 1])
+            produce(4 * m + k + 1, *bufs[2 * ((k + 1) % 2):2 * ((k + 1) % 2) + 2])
+        return 0
+    lax.fori_loop(0, BLOCKS, step, 0)
+
+
+def pass_kernel(final, base, own, slab_a, slab_b, tile_a, tile_b, out,
                 cols, blocks, lhs, tiles, select, res, *bufs):
     center_blocks(own, blocks)
+    odd_s = lax.axis_index("slab") % 2
+    odd_t = lax.axis_index("tile") % 2
+    x_a, y_a = 3 - 3 * odd_s, 3 - 3 * odd_t
+    x_b, y_b = 3 - x_a, 3 - y_a
     for i in range(2):
         for y in range(2):
             cols[4 * (i + 1) + y + 1] = own[2 * i + y]
-        cols[1 + i] = low[i]
-        cols[13 + i] = high[i]
-    for i in range(4):
-        cols[4 * i] = front[i]
-        cols[4 * i + 3] = back[i]
+        cols[4 * x_a + 1 + i] = slab_a[i]
+        cols[4 * x_b + 1 + i] = slab_b[i]
+    for ref, y in ((tile_a, y_a), (tile_b, y_b)):
+        cols[4 * x_a + y] = ref[0]
+        cols[4 + y] = ref[1]
+        cols[8 + y] = ref[2]
+        cols[4 * x_b + y] = ref[3]
 
     def one(j, _):
         column_features(cols.at[j], (j // 4).astype(jnp.float32) - 1.5,
@@ -292,11 +296,26 @@
     lax.fori_loop(0, 4, finish, 0)
 
 
+def swapped(value, axis, first):
+    count = lax.axis_size(axis)
+    trades = []
+    for i in range(first, count - 1, 2):
+        trades += [(i, i + 1), (i + 1, i)]
+    return lax.ppermute(value, axis, trades)
+
+
 def rates_pass(final, base, own):
-    low = shifted(own[2:4], "slab", 1)
-    high = shifted(own[0:2], "slab", -1)
-    front = shifted(jnp.concatenate([low[1:2], own[1:2], own[3:4], high[1:2]]), "tile", 1)
-    back = shifted(jnp.concatenate([low[0:1], own[0:1], own[2:3], high[0:1]]), "tile", -1)
+    odd_s = lax.axis_index("slab") % 2
+    odd_t = lax.axis_index("tile") % 2
+    grid = own.reshape(2, 2, BLOCKS, 8, 128)
+    slabs = [swapped(lax.dynamic_index_in_dim(grid, (1 - odd_s + k) % 2, 0, False), "slab", k)
+             for k in range(2)]
+
+    def edge(k):
+        at = (1 - odd_t + k) % 2
+        four = jnp.stack([slabs[0], grid[0], grid[1], slabs[1]])
+        return lax.dynamic_index_in_dim(four, at, 1, False)
+    tiles = [swapped(edge(k), "tile", k) for k in range(2)]
 
     def body(*refs):
         pass_kernel(final, *refs)
@@ -313,7 +332,7 @@
                         *work, *work],
         compiler_params=pltpu.CompilerParams(vmem_limit_bytes=40 << 20),
         name="correct_pass" if final else "predict_pass",
-    )(base, own, low, high, front, back)
+    )(base, own, *slabs, *tiles)
 
 
 def slot_mask(cell_counts):
@@ -336,12 +355,6 @@
     return jnp.take(flat_face, source_row, axis=1)
 
 
-def shifted(value, axis, steps):
-    count = lax.axis_size(axis)
-    leading, last = (max(0, -steps), min(count, count - steps))
-    return lax.ppermute(value, axis, [(source, source + steps) for source in range(leading, last)])
-
-
 def start_fields(particles, counts):
     mask = slot_mask(counts).reshape(2, 2, CZ * SLOTS)
     dens = jnp.where(mask, particles[6], 1.0)
@@ -363,9 +376,10 @@
     kept = jnp.where(slot_mask(remain).reshape(1, 2, 2, CZ * SLOTS), updated, 0.0)
     lower_rows = pack_leavers(updated[:, 0], counts[0], leavers[0, 0])
     upper_rows = pack_leavers(updated[:, 1], counts[1], leavers[1, 0])
-    from_below = shifted(upper_rows, "slab", 1)
-    from_above = shifted(lower_rows, "slab", -1)
-    return (kept, jnp.stack([from_below, from_above], axis=0))
+    odd = lax.axis_index("slab") % 2 == 1
+    first = swapped(jnp.where(odd, lower_rows, upper_rows), "slab", 0)
+    second = swapped(jnp.where(odd, upper_rows, lower_rows), "slab", 1)
+    return (kept, jnp.stack([jnp.where(odd, first, second), jnp.where(odd, second, first)]))
 
 
 def solution(mesh):

time: 127 us -> 114 us (0.90)
  starting transfers between devices: 38.3 us -> 27 us
  Pallas kernels: 59.7 us -> 55.5 us
  waiting for transfers between devices: 18 us -> 21.2 us
    ppermute x10, starting transfers between devices: 38.3 us -> 27 us  [swapped(): return lax.ppermute(value, axis, trades)]
    pallas_call x2, Pallas kernels: 59.7 us -> 55.5 us  [rates_pass(): pl.pallas_call(body, out_shape=jax.ShapeDtypeStruct((4, BLOCKS, 8, 128),...]
    ppermute x10, waiting for transfers between devices: 18 us -> 21.2 us  [swapped(): return lax.ppermute(value, axis, trades)]
  transfers between devices with their start and end apart: 10 -> 10, of which waited for: 8 -> 8; matrix products, arithmetic and copies ran while one was open for 3% -> 2% of each run, Pallas kernels for 0% -> 0%
where the time goes in v3:
time: 114 us
  Pallas kernels  55.5 us (49%)
  starting transfers between devices  27 us (24%)
  waiting for transfers between devices  21.2 us (19%)
  local copies, waits for them, and re-layouts  5.93 us (5%)
  other arithmetic  3.3 us (3%)
    pallas_call x2, Pallas kernels, rates_pass(): pl.pallas_call(body, out_shape=jax.ShapeDtypeStruct((4, BLOCKS, 8, 128),...  55.5 us
    ppermute x10, starting transfers between devices, swapped(): return lax.ppermute(value, axis, trades)  27 us
    ppermute x10, waiting for transfers between devices, swapped(): return lax.ppermute(value, axis, trades)  21.2 us
  transfers between devices with their start and end apart: 10, of which 8 were waited for; matrix products, arithmetic and copies ran while one was open for 2% of the time, Pallas kernels for 0%

profile of v3, /device:TPU:10, one launch (start us, length us, event | category | flops | bytes accessed | tf_op | source)
XLA Modules:
  0.0 113.9 jit_solution(4601286335467173158)
XLA Ops:
  0.6 0.7 copy.36
  1.4 0.1 lt.108
  1.5 0.1 lt.106
  1.8 1.1 concatenate.12
  2.8 0.8 multiply_divide_fusion
  3.7 0.1 copy.25
  3.9 4.2 %collective-permute-start.1 = (f32[2,12,8,128]{3,2,1,0:T(8,128)S(1)}, f32[2,12,8,128]{3,2,1,0:T(8,128)S(1)}, u32[]{:S(2)}, u32[]{:S(2)}) collective-permute-start(f32[2,12,8,128]{3,2,1,0:T(8,128)S(1)} %get-tuple-element.49), channel_id=1, source_target_pairs={{16,32},{32,16},{48,64},{64,48},{80,96},{96,80},{17,33},{33,17},{4... | collective-permute-start | bytes 294920 | tf_op jit(solution)/shard_map/ppermute | solution.py:304
  8.1 2.3 %collective-permute-start = (f32[2,12,8,128]{3,2,1,0:T(8,128)S(1)}, f32[2,12,8,128]{3,2,1,0:T(8,128)S(1)}, u32[]{:S(2)}, u32[]{:S(2)}) collective-permute-start(f32[2,12,8,128]{3,2,1,0:T(8,128)S(1)} %get-tuple-element.50), channel_id=1, source_target_pairs={{0,16},{16,0},{32,48},{48,32},{64,80},{80,64},{96,112},{112,96},{1... | collective-permute-start | bytes 294920 | tf_op jit(solution)/shard_map/ppermute | solution.py:304
  10.4 0.1 reshape_squeeze.22
  10.5 0.1 reshape.261
  10.6 0.1 reshape_squeeze.19
  10.7 0.1 reshape.260
  10.9 0.1 reduce-window.15
  11.0 0.1 reduce.5
  11.1 0.1 reduce-window.14
  11.3 0.1 reduce.4
  11.4 0.1 reshape_squeeze.20
  11.5 0.1 lt.102
  11.6 0.1 lt.103
  11.8 0.1 select_reduce_fusion.1
  12.0 0.1 select_reduce_fusion
  12.1 0.8 collective-permute-done.1.refs_3_
  12.9 2.0 %collective-permute-done.refs_2_ = f32[2,12,8,128]{3,2,1,0:T(8,128)S(1)} collective-permute-done((f32[2,12,8,128]{3,2,1,0:T(8,128)S(1)}, f32[2,12,8,128]{3,2,1,0:T(8,128)S(1)}, u32[]{:S(2)}, u32[]{:S(2)}) %collective-permute-start) | collective-permute-done | bytes 98336 | tf_op jit(solution)/shard_map/ppermute | solution.py:304
  15.0 4.6 %collective-permute-start.3 = (f32[4,12,8,128]{3,2,1,0:T(8,128)S(1)}, f32[4,12,8,128]{3,2,1,0:T(8,128)S(1)}, u32[]{:S(2)}, u32[]{:S(2)}) collective-permute-start(f32[4,12,8,128]{3,2,1,0:T(8,128)S(1)} %get-tuple-element.37), channel_id=1, source_target_pairs={{1,2},{2,1},{3,4},{4,3},{5,6},{6,5},{7,8},{8,7},{9,10},{10,9},{11,... | collective-permute-start | bytes 589832 | tf_op jit(solution)/shard_map/ppermute | solution.py:304
  19.6 0.1 collective-permute-start.2
  19.7 4.4 %collective-permute-done.3.refs_5_ = f32[4,12,8,128]{3,2,1,0:T(8,128)S(1)} collective-permute-done((f32[4,12,8,128]{3,2,1,0:T(8,128)S(1)}, f32[4,12,8,128]{3,2,1,0:T(8,128)S(1)}, u32[]{:S(2)}, u32[]{:S(2)}) %collective-permute-start.3) | collective-permute-done | bytes 196640 | tf_op jit(solution)/shard_map/ppermute | solution.py:304
  24.1 27.8 %predict_pass.1.refs_1_ = f32[4,12,8,128]{3,2,1,0:T(8,128)S(1)} custom-call(f32[4,12,8,128]{3,2,1,0:T(8,128)S(1)} %fusion.8.refs_0_.refs_1_, f32[4,12,8,128]{3,2,1,0:T(8,128)S(1)} %fusion.8.refs_0_.refs_1_, f32[2,12,8,128]{3,2,1,0:T(8,128)S(1)} %collective-permute-done.refs_2_, f32[2,12,8,128]{3,2,1,0:T(8,128)S(1)} %collective-permute-done.1.refs_3_, ...), custom_call_target="tpu_custom_call" | custom-call | tf_op jit(solution)/shard_map/predict_pass/pallas_call | solution.py:323
  51.9 4.1 %collective-permute-start.5 = (f32[2,12,8,128]{3,2,1,0:T(8,128)S(1)}, f32[2,12,8,128]{3,2,1,0:T(8,128)S(1)}, u32[]{:S(2)}, u32[]{:S(2)}) collective-permute-start(f32[2,12,8,128]{3,2,1,0:T(8,128)S(1)} %get-tuple-element.45), channel_id=1, source_target_pairs={{16,32},{32,16},{48,64},{64,48},{80,96},{96,80},{17,33},{33,17},{4... | collective-permute-start | bytes 294920 | tf_op jit(solution)/shard_map/ppermute | solution.py:304
  56.1 2.3 %collective-permute-start.4 = (f32[2,12,8,128]{3,2,1,0:T(8,128)S(1)}, f32[2,12,8,128]{3,2,1,0:T(8,128)S(1)}, u32[]{:S(2)}, u32[]{:S(2)}) collective-permute-start(f32[2,12,8,128]{3,2,1,0:T(8,128)S(1)} %get-tuple-element.46), channel_id=1, source_target_pairs={{0,16},{16,0},{32,48},{48,32},{64,80},{80,64},{96,112},{112,96},{1... | collective-permute-start | bytes 294920 | tf_op jit(solution)/shard_map/ppermute | solution.py:304
  58.4 2.5 %collective-permute-done.5.refs_3_ = f32[2,12,8,128]{3,2,1,0:T(8,128)S(1)} collective-permute-done((f32[2,12,8,128]{3,2,1,0:T(8,128)S(1)}, f32[2,12,8,128]{3,2,1,0:T(8,128)S(1)}, u32[]{:S(2)}, u32[]{:S(2)}) %collective-permute-start.5) | collective-permute-done | bytes 98336 | tf_op jit(solution)/shard_map/ppermute | solution.py:304
  60.8 1.4 %collective-permute-done.4.refs_2_ = f32[2,12,8,128]{3,2,1,0:T(8,128)S(1)} collective-permute-done((f32[2,12,8,128]{3,2,1,0:T(8,128)S(1)}, f32[2,12,8,128]{3,2,1,0:T(8,128)S(1)}, u32[]{:S(2)}, u32[]{:S(2)}) %collective-permute-start.4) | collective-permute-done | bytes 98336 | tf_op jit(solution)/shard_map/ppermute | solution.py:304
  62.4 5.1 %collective-permute-start.7 = (f32[4,12,8,128]{3,2,1,0:T(8,128)S(1)}, f32[4,12,8,128]{3,2,1,0:T(8,128)S(1)}, u32[]{:S(2)}, u32[]{:S(2)}) collective-permute-start(f32[4,12,8,128]{3,2,1,0:T(8,128)S(1)} %get-tuple-element.35), channel_id=1, source_target_pairs={{1,2},{2,1},{3,4},{4,3},{5,6},{6,5},{7,8},{8,7},{9,10},{10,9},{11,... | collective-permute-start | bytes 589832 | tf_op jit(solution)/shard_map/ppermute | solution.py:304
  67.5 0.1 collective-permute-start.6
  67.6 3.9 %collective-permute-done.7.refs_5_ = f32[4,12,8,128]{3,2,1,0:T(8,128)S(1)} collective-permute-done((f32[4,12,8,128]{3,2,1,0:T(8,128)S(1)}, f32[4,12,8,128]{3,2,1,0:T(8,128)S(1)}, u32[]{:S(2)}, u32[]{:S(2)}) %collective-permute-start.7) | collective-permute-done | bytes 196640 | tf_op jit(solution)/shard_map/ppermute | solution.py:304
  71.5 27.7 %correct_pass.1 = f32[4,12,8,128]{3,2,1,0:T(8,128)S(1)} custom-call(f32[4,12,8,128]{3,2,1,0:T(8,128)S(1)} %fusion.8.refs_0_.refs_1_, f32[4,12,8,128]{3,2,1,0:T(8,128)S(1)} %predict_pass.1.refs_1_, f32[2,12,8,128]{3,2,1,0:T(8,128)S(1)} %collective-permute-done.4.refs_2_, f32[2,12,8,128]{3,2,1,0:T(8,128)S(1)} %collective-permute-done.5.refs_3_, ...), custom_call_target="tpu_custom_call" | custom-call | tf_op jit(solution)/shard_map/correct_pass/pallas_call | solution.py:323
  99.2 0.1 reshape.233
  99.4 0.5 copy.28
  99.9 0.5 copy.30
  100.4 0.7 gather_fusion
  101.1 0.7 gather_fusion.1
  101.8 0.1 bitcast_select_fusion.1
  101.9 2.3 %collective-permute-start.8 = (f32[7,192]{0,1:T(8,128)S(1)}, f32[7,192]{0,1:T(8,128)S(1)}, u32[]{:S(2)}, u32[]{:S(2)}) collective-permute-start(f32[7,192]{0,1:T(8,128)S(1)} %get-tuple-element.39), channel_id=1, source_target_pairs={{0,16},{16,0},{32,48},{48,32},{64,80},{80,64},{96,112},{112,96},{1... | collective-permute-start | bytes 16136 | tf_op jit(solution)/shard_map/ppermute | solution.py:304
  104.2 1.9 %collective-permute-start.9 = (f32[7,192]{0,1:T(8,128)S(1)}, f32[7,192]{0,1:T(8,128)S(1)}, u32[]{:S(2)}, u32[]{:S(2)}) collective-permute-start(f32[7,192]{0,1:T(8,128)S(1)} %get-tuple-element.40), channel_id=1, source_target_pairs={{16,32},{32,16},{48,64},{64,48},{80,96},{96,80},{17,33},{33,17},{4... | collective-permute-start | bytes 16136 | tf_op jit(solution)/shard_map/ppermute | solution.py:304
  106.1 0.8 broadcast_select_fusion
  106.9 1.2 %collective-permute-done.8 = f32[7,192]{0,1:T(8,128)S(1)} collective-permute-done((f32[7,192]{0,1:T(8,128)S(1)}, f32[7,192]{0,1:T(8,128)S(1)}, u32[]{:S(2)}, u32[]{:S(2)}) %collective-permute-start.8) | collective-permute-done | bytes 5408 | tf_op jit(solution)/shard_map/ppermute | solution.py:304
  108.1 5.0 %collective-permute-done.9 = f32[7,192]{0,1:T(8,128)S(1)} collective-permute-done((f32[7,192]{0,1:T(8,128)S(1)}, f32[7,192]{0,1:T(8,128)S(1)}, u32[]{:S(2)}, u32[]{:S(2)}) %collective-permute-start.9) | collective-permute-done | bytes 5408 | tf_op jit(solution)/shard_map/ppermute | solution.py:304
  113.2 0.1 copy.32
  113.3 0.6 pad_maximum_fusion.2
  (36 shorter events, 0.9 us)
Async XLA Ops:
  0.6 9.7 %copy-start = (s32[2,1,2,48]{3,2,1,0:T(2,128)S(1)}, s32[2,1,2,48]{3,2,1,0:T(2,128)}, u32[]{:S(2)}) copy-start(s32[2,1,2,48]{3,2,1,0:T(2,128)} %param.11) | copy-start | bytes 2308
  3.9 9.0 %collective-permute-start.1 = (f32[2,12,8,128]{3,2,1,0:T(8,128)S(1)}, f32[2,12,8,128]{3,2,1,0:T(8,128)S(1)}, u32[]{:S(2)}, u32[]{:S(2)}) collective-permute-start(f32[2,12,8,128]{3,2,1,0:T(8,128)S(1)} %get-tuple-element.49), channel_id=1, source_target_pairs={{16,32},{32,16},{48,64},{64,48},{80,96},{96,80},{17,33},{33,17},{4... | collective-permute-start | bytes 294920 | tf_op jit(solution)/shard_map/ppermute | solution.py:304
  8.1 6.8 %collective-permute-start = (f32[2,12,8,128]{3,2,1,0:T(8,128)S(1)}, f32[2,12,8,128]{3,2,1,0:T(8,128)S(1)}, u32[]{:S(2)}, u32[]{:S(2)}) collective-permute-start(f32[2,12,8,128]{3,2,1,0:T(8,128)S(1)} %get-tuple-element.50), channel_id=1, source_target_pairs={{0,16},{16,0},{32,48},{48,32},{64,80},{80,64},{96,112},{112,96},{1... | collective-permute-start | bytes 294920 | tf_op jit(solution)/shard_map/ppermute | solution.py:304
  15.0 9.1 %collective-permute-start.3 = (f32[4,12,8,128]{3,2,1,0:T(8,128)S(1)}, f32[4,12,8,128]{3,2,1,0:T(8,128)S(1)}, u32[]{:S(2)}, u32[]{:S(2)}) collective-permute-start(f32[4,12,8,128]{3,2,1,0:T(8,128)S(1)} %get-tuple-element.37), channel_id=1, source_target_pairs={{1,2},{2,1},{3,4},{4,3},{5,6},{6,5},{7,8},{8,7},{9,10},{10,9},{11,... | collective-permute-start | bytes 589832 | tf_op jit(solution)/shard_map/ppermute | solution.py:304
  19.6 4.5 %collective-permute-start.2 = (f32[4,12,8,128]{3,2,1,0:T(8,128)S(1)}, f32[4,12,8,128]{3,2,1,0:T(8,128)S(1)}, u32[]{:S(2)}, u32[]{:S(2)}) collective-permute-start(f32[4,12,8,128]{3,2,1,0:T(8,128)S(1)} %get-tuple-element.38), channel_id=1, source_target_pairs={{0,1},{1,0},{2,3},{3,2},{4,5},{5,4},{6,7},{7,6},{8,9},{9,8},{10,11... | collective-permute-start | bytes 589832 | tf_op jit(solution)/shard_map/ppermute | solution.py:304
  51.9 8.9 %collective-permute-start.5 = (f32[2,12,8,128]{3,2,1,0:T(8,128)S(1)}, f32[2,12,8,128]{3,2,1,0:T(8,128)S(1)}, u32[]{:S(2)}, u32[]{:S(2)}) collective-permute-start(f32[2,12,8,128]{3,2,1,0:T(8,128)S(1)} %get-tuple-element.45), channel_id=1, source_target_pairs={{16,32},{32,16},{48,64},{64,48},{80,96},{96,80},{17,33},{33,17},{4... | collective-permute-start | bytes 294920 | tf_op jit(solution)/shard_map/ppermute | solution.py:304
  56.1 6.2 %collective-permute-start.4 = (f32[2,12,8,128]{3,2,1,0:T(8,128)S(1)}, f32[2,12,8,128]{3,2,1,0:T(8,128)S(1)}, u32[]{:S(2)}, u32[]{:S(2)}) collective-permute-start(f32[2,12,8,128]{3,2,1,0:T(8,128)S(1)} %get-tuple-element.46), channel_id=1, source_target_pairs={{0,16},{16,0},{32,48},{48,32},{64,80},{80,64},{96,112},{112,96},{1... | collective-permute-start | bytes 294920 | tf_op jit(solution)/shard_map/ppermute | solution.py:304
  62.4 9.1 %collective-permute-start.7 = (f32[4,12,8,128]{3,2,1,0:T(8,128)S(1)}, f32[4,12,8,128]{3,2,1,0:T(8,128)S(1)}, u32[]{:S(2)}, u32[]{:S(2)}) collective-permute-start(f32[4,12,8,128]{3,2,1,0:T(8,128)S(1)} %get-tuple-element.35), channel_id=1, source_target_pairs={{1,2},{2,1},{3,4},{4,3},{5,6},{6,5},{7,8},{8,7},{9,10},{10,9},{11,... | collective-permute-start | bytes 589832 | tf_op jit(solution)/shard_map/ppermute | solution.py:304
  67.5 4.0 %collective-permute-start.6 = (f32[4,12,8,128]{3,2,1,0:T(8,128)S(1)}, f32[4,12,8,128]{3,2,1,0:T(8,128)S(1)}, u32[]{:S(2)}, u32[]{:S(2)}) collective-permute-start(f32[4,12,8,128]{3,2,1,0:T(8,128)S(1)} %get-tuple-element.36), channel_id=1, source_target_pairs={{0,1},{1,0},{2,3},{3,2},{4,5},{5,4},{6,7},{7,6},{8,9},{9,8},{10,11... | collective-permute-start | bytes 589832 | tf_op jit(solution)/shard_map/ppermute | solution.py:304
  101.9 6.2 %collective-permute-start.8 = (f32[7,192]{0,1:T(8,128)S(1)}, f32[7,192]{0,1:T(8,128)S(1)}, u32[]{:S(2)}, u32[]{:S(2)}) collective-permute-start(f32[7,192]{0,1:T(8,128)S(1)} %get-tuple-element.39), channel_id=1, source_target_pairs={{0,16},{16,0},{32,48},{48,32},{64,80},{80,64},{96,112},{112,96},{1... | collective-permute-start | bytes 16136 | tf_op jit(solution)/shard_map/ppermute | solution.py:304
  104.2 8.9 %collective-permute-start.9 = (f32[7,192]{0,1:T(8,128)S(1)}, f32[7,192]{0,1:T(8,128)S(1)}, u32[]{:S(2)}, u32[]{:S(2)}) collective-permute-start(f32[7,192]{0,1:T(8,128)S(1)} %get-tuple-element.40), channel_id=1, source_target_pairs={{16,32},{32,16},{48,64},{64,48},{80,96},{96,80},{17,33},{33,17},{4... | collective-permute-start | bytes 16136 | tf_op jit(solution)/shard_map/ppermute | solution.py:304

commit v4 on v3

--- a/solution.py
+++ b/solution.py
@@ -26,6 +26,7 @@
 visc_gain = 2.0 * viscosity * sound_speed * smoothing
 FAR = 2.0**50
 MIDDLE = 5.5
+UNROLL = 12
 SPAN = 32 * (BLOCKS + 2)
 AROUND = (0, 1, 2, 4, 5, 6, 8, 9, 10)
 
@@ -55,10 +56,13 @@
     for k, part in enumerate(pieces(square) + pieces(flow)):
         tail = jnp.where(sub == k, part, tail)
     last = jnp.where(sub == 0, 1.0, 0.0)
-    return [high, high, mid, high, low, mid, tail, last]
-
-
-def column_features(src, far_x, far_y, col, lhs):
+    turned = pltpu.roll(low, 6, 0)
+    places = [jnp.where(sub < 3, high, jnp.where(sub < 6, pltpu.roll(mid, 3, 0), turned)),
+              jnp.where(sub == 0, turned, jnp.where(sub == 1, 1.0, 0.0))]
+    return [high, high, mid, high, low, mid, tail, last], places
+
+
+def column_features(src, far_x, far_y, col, lhs, places):
     sub = lax.broadcasted_iota(jnp.int32, (8, 128), 0)
     chunk = lax.broadcasted_iota(jnp.int32, (8, 128), 1) // 32
     for beta in range(4):
@@ -73,7 +77,11 @@
                 above = src[3 * g + 3] if g < 3 else none
                 vals = jnp.where(chunk == 3, below, jnp.where(chunk == 0, above, 0.0))
                 level = jnp.where(chunk == 3, -1.0, 12.0)
-            rows += neighbour_rows(vals, far_x, far_y, level - MIDDLE, sub)
+            more, put = neighbour_rows(vals, far_x, far_y, level - MIDDLE, sub)
+            rows += more
+            put = jnp.concatenate(put, axis=0).astype(jnp.bfloat16)
+            for tile in ((beta + 1,) if beta < 3 else (0, 4)):
+                places[col, tile, 16 * g:16 * g + 16] = put
         for h in range(2):
             flat = jnp.concatenate(rows[16 * h:16 * h + 16], axis=0).T.astype(jnp.bfloat16)
             lanes = slice(128 * h, 128 * h + 128)
@@ -82,24 +90,6 @@
             else:
                 lhs[col, 0:32, lanes] = flat[96:128]
                 lhs[col, 416:448, lanes] = flat[0:32]
-
-
-def spread_positions(count, lhs, select, tiles):
-    k = lax.broadcasted_iota(jnp.int32, (256, 384), 0)
-    n = lax.broadcasted_iota(jnp.int32, (256, 384), 1)
-    part = k % 64
-    hit = (part % 8 == n // 128) & ((part // 8) % 2 == 0) & (part < 40) & (k // 64 == (n % 128) // 32)
-    select[...] = jnp.where(hit, 1.0, 0.0).astype(jnp.bfloat16)
-
-    def four(n, _):
-        rows = lhs[pl.ds(4 * n, 4)].reshape(4 * SPAN, 256)
-        out = jnp.dot(rows, select[...], preferred_element_type=jnp.float32)
-        for c in range(4):
-            for f in range(3):
-                part = out[SPAN * c:SPAN * (c + 1), 128 * f:128 * f + 128]
-                tiles[4 * n + c, f] = part.reshape(SPAN // 8, 8, 128)
-        return 0
-    lax.fori_loop(0, count // 4, four, 0)
 
 
 def swap_chunks(load, store):
@@ -175,15 +165,13 @@
                 weights[row:row + 16, 128 * n:128 * n + 128] = part * mask
 
 
-def pair(acc, terms, tile):
+def pair(drift, terms):
     r2, approach, dens, ratio = terms
     r2 = jnp.maximum(r2, 1e-30)
     support = jnp.maximum(1.0 - r2 * lax.rsqrt(r2), 0.0)
     slope = support * support * support
     visc = jnp.maximum(approach, 0.0) / ((r2 + visc_floor) * dens)
-    force = (ratio + visc) * slope
-    return (acc[0] + force * tile[0], acc[1] + force * tile[1], acc[2] + force * tile[2],
-            acc[3] + slope * approach, acc[4] + force)
+    return drift + slope * approach, (ratio + visc) * slope
 
 
 def center_blocks(own, blocks):
@@ -202,7 +190,10 @@
     lax.fori_loop(0, 4, one, 0)
 
 
-def all_pairs(blocks, lhs, tiles, bufs, emit):
+def all_pairs(blocks, lhs, places, bufs, forces, drifts, emit):
+    chunk = lax.broadcasted_iota(jnp.int32, (8, 128), 1) // 32
+    wide = lax.broadcasted_iota(jnp.int32, (64, 128), 1) // 32
+
     def first_column(c):
         return 4 * (c // 2) + c % 2
 
@@ -214,33 +205,72 @@
         near = jnp.concatenate([lhs[first_column(c) + j, rows, :] for j in AROUND], axis=0)
         result[...] = jnp.dot(near, weights[...], preferred_element_type=jnp.float32)
 
-    def consume(n, result):
+    def consume(k, result):
+        drift = jnp.zeros((8, 128), jnp.float32)
+        for j in range(9):
+            for d in range(3):
+                for h in range(2):
+                    both = []
+                    for i in range(2):
+                        r = 96 * j + 32 * d + 16 * h + 8 * i
+                        terms = [result[r:r + 8, 128 * n:128 * n + 128] for n in range(4)]
+                        drift, force = pair(drift, terms)
+                        both.append(force)
+                    full = jnp.concatenate(both, axis=0)
+                    top = full.astype(jnp.bfloat16)
+                    r = 128 * j + 32 * ((k - 1 + d) % 4) + 16 * h
+                    forces[k, r:r + 16, 0:128] = top
+                    forces[k, r:r + 16, 128:256] = (full - top.astype(jnp.float32)).astype(
+                        jnp.bfloat16)
+        drifts[k] = drift
+
+    def reduce(n, k):
+        n = jnp.maximum(n, 0)
         c, b = n // BLOCKS, n % BLOCKS
-        acc = tuple(jnp.zeros((8, 128), jnp.float32) for _ in range(5))
-        for k, j in enumerate(AROUND):
-            for i in range(12):
-                r = 96 * k + 8 * i
-                terms = [result[r:r + 8, 128 * n:128 * n + 128] for n in range(4)]
-                acc = pair(acc, terms, [tiles[first_column(c) + j, f, 4 * b + i] for f in range(3)])
-        sums = [jnp.sum(a, axis=0, keepdims=True) for a in acc]
+        tile = b // 4 + 1
+        parts = []
+        for j in AROUND:
+            col = first_column(c) + j
+            part = places[col, tile]
+            if k == 0:
+                part = jnp.where(wide == 3, places[col, tile - 1], part)
+            if k == 3:
+                part = jnp.where(wide == 0, places[col, tile + 1], part)
+            parts.append(part)
+        out = jnp.dot(jnp.concatenate(parts, axis=1), forces[k], preferred_element_type=jnp.float32)
+        out = out[:, 0:128] + out[:, 128:256]
+        first, second = out[0:8], out[8:16]
+        for g in range(1, 4):
+            first = jnp.where(chunk == g, out[16 * g:16 * g + 8], first)
+            second = jnp.where(chunk == g, out[16 * g + 8:16 * g + 16], second)
+        force = second[1:2]
+        moments = [first[0:1] + first[3:4] + first[6:7], first[1:2] + first[4:5] + first[7:8],
+                   first[2:3] + first[5:6] + second[0:1]]
         rows = blocks[c, b]
-        sums = [rows[k:k + 1] * sums[4] - sums[k] for k in range(3)] + sums[3:4]
+        sums = [rows[f:f + 1] * force - moments[f] for f in range(3)]
+        sums.append(jnp.sum(drifts[k], axis=0, keepdims=True))
         emit(c, b, jnp.concatenate(sums + [jnp.zeros((4, 128), jnp.float32)], axis=0))
 
     fill_weights(bufs[0])
     fill_weights(bufs[2])
     produce(0, *bufs[:2])
+    for k in range(4):
+        for j in range(9):
+            r = 128 * j + 32 * ((k + 2) % 4)
+            forces[k, r:r + 32] = jnp.zeros((32, 256), jnp.bfloat16)
 
     def step(m, _):
-        for k in range(4):
-            consume(4 * m + k, bufs[2 * (k % 2) + 1])
-            produce(4 * m + k + 1, *bufs[2 * ((k + 1) % 2):2 * ((k + 1) % 2) + 2])
+        for k in range(UNROLL):
+            consume(k % 4, bufs[2 * (k % 2) + 1])
+            produce(UNROLL * m + k + 1, *bufs[2 * ((k + 1) % 2):2 * ((k + 1) % 2) + 2])
+            reduce(UNROLL * m + k - 1, (k - 1) % 4)
         return 0
-    lax.fori_loop(0, BLOCKS, step, 0)
+    lax.fori_loop(0, 4 * BLOCKS // UNROLL, step, 0)
+    reduce(4 * BLOCKS - 1, 3)
 
 
 def pass_kernel(final, base, own, slab_a, slab_b, tile_a, tile_b, out,
-                cols, blocks, lhs, tiles, select, res, *bufs):
+                cols, blocks, lhs, places, res, forces, drifts, *bufs):
     center_blocks(own, blocks)
     odd_s = lax.axis_index("slab") % 2
     odd_t = lax.axis_index("tile") % 2
@@ -259,14 +289,13 @@
 
     def one(j, _):
         column_features(cols.at[j], (j // 4).astype(jnp.float32) - 1.5,
-                        (j % 4).astype(jnp.float32) - 1.5, j, lhs)
+                        (j % 4).astype(jnp.float32) - 1.5, j, lhs, places)
         return 0
     lax.fori_loop(0, 16, one, 0)
-    spread_positions(16, lhs, select, tiles)
 
     def emit(c, b, sums):
         res[c, b] = sums
-    all_pairs(blocks, lhs, tiles, bufs, emit)
+    all_pairs(blocks, lhs, places, bufs, forces, drifts, emit)
 
     def finish(c, _):
         def store(r, rates):
@@ -326,9 +355,10 @@
         scratch_shapes=[pltpu.VMEM((16, BLOCKS, 8, 128), jnp.float32),
                         pltpu.VMEM((4, BLOCKS, 8, 128), jnp.float32),
                         pltpu.VMEM((16, SPAN, 256), jnp.bfloat16),
-                        pltpu.VMEM((16, 3, SPAN // 8, 8, 128), jnp.float32),
-                        pltpu.VMEM((256, 384), jnp.bfloat16),
+                        pltpu.VMEM((16, 5, 64, 128), jnp.bfloat16),
                         pltpu.VMEM((4, BLOCKS, 8, 128), jnp.float32),
+                        pltpu.VMEM((4, 1152, 256), jnp.bfloat16),
+                        pltpu.VMEM((4, 8, 128), jnp.float32),
                         *work, *work],
         compiler_params=pltpu.CompilerParams(vmem_limit_bytes=40 << 20),
         name="correct_pass" if final else "predict_pass",

time: 114 us -> 112 us (0.982)
  Pallas kernels: 55.5 us -> 53.1 us
    pallas_call x2, Pallas kernels: 55.5 us -> 53.1 us  [rates_pass(): pl.pallas_call(body, out_shape=jax.ShapeDtypeStruct((4, BLOCKS, 8, 128),...]
where the time goes in v4:
time: 112 us; the launch traced here: 111 us
  Pallas kernels  53.1 us (47%)
  starting transfers between devices  27.2 us (24%)
  waiting for transfers between devices  20.9 us (19%)
  local copies, waits for them, and re-layouts  5.93 us (5%)
  other arithmetic  3.3 us (3%)
    pallas_call x2, Pallas kernels, rates_pass(): pl.pallas_call(body, out_shape=jax.ShapeDtypeStruct((4, BLOCKS, 8, 128),...  53.1 us
    ppermute x10, starting transfers between devices, swapped(): return lax.ppermute(value, axis, trades)  27.2 us
    ppermute x10, waiting for transfers between devices, swapped(): return lax.ppermute(value, axis, trades)  20.9 us
  transfers between devices with their start and end apart: 10, of which 8 were waited for; matrix products, arithmetic and copies ran while one was open for 2% of the time, Pallas kernels for 0%

profile of v4, /device:TPU:10, one launch (start us, length us, event | category | flops | bytes accessed | tf_op | source)
XLA Modules:
  0.0 111.5 jit_solution(5274227555339129806)
XLA Ops:
  0.6 0.7 copy.36
  1.4 0.1 lt.108
  1.5 0.1 lt.106
  1.8 1.1 concatenate.12
  2.8 0.8 multiply_divide_fusion
  3.7 0.1 copy.25
  3.9 4.2 %collective-permute-start.1 = (f32[2,12,8,128]{3,2,1,0:T(8,128)S(1)}, f32[2,12,8,128]{3,2,1,0:T(8,128)S(1)}, u32[]{:S(2)}, u32[]{:S(2)}) collective-permute-start(f32[2,12,8,128]{3,2,1,0:T(8,128)S(1)} %get-tuple-element.49), channel_id=1, source_target_pairs={{16,32},{32,16},{48,64},{64,48},{80,96},{96,80},{17,33},{33,17},{4... | collective-permute-start | bytes 294920 | tf_op jit(solution)/shard_map/ppermute | solution.py:333
  8.1 2.3 %collective-permute-start = (f32[2,12,8,128]{3,2,1,0:T(8,128)S(1)}, f32[2,12,8,128]{3,2,1,0:T(8,128)S(1)}, u32[]{:S(2)}, u32[]{:S(2)}) collective-permute-start(f32[2,12,8,128]{3,2,1,0:T(8,128)S(1)} %get-tuple-element.50), channel_id=1, source_target_pairs={{0,16},{16,0},{32,48},{48,32},{64,80},{80,64},{96,112},{112,96},{1... | collective-permute-start | bytes 294920 | tf_op jit(solution)/shard_map/ppermute | solution.py:333
  10.4 0.1 reshape_squeeze.22
  10.5 0.1 reshape.261
  10.6 0.1 reshape_squeeze.19
  10.7 0.1 reshape.260
  10.9 0.1 reduce-window.15
  11.0 0.1 reduce.5
  11.1 0.1 reduce-window.14
  11.3 0.1 reduce.4
  11.4 0.1 reshape_squeeze.20
  11.5 0.1 lt.102
  11.6 0.1 lt.103
  11.8 0.1 select_reduce_fusion.1
  12.0 0.1 select_reduce_fusion
  12.1 0.8 collective-permute-done.1.refs_3_
  12.9 2.0 %collective-permute-done.refs_2_ = f32[2,12,8,128]{3,2,1,0:T(8,128)S(1)} collective-permute-done((f32[2,12,8,128]{3,2,1,0:T(8,128)S(1)}, f32[2,12,8,128]{3,2,1,0:T(8,128)S(1)}, u32[]{:S(2)}, u32[]{:S(2)}) %collective-permute-start) | collective-permute-done | bytes 98336 | tf_op jit(solution)/shard_map/ppermute | solution.py:333
  15.0 4.6 %collective-permute-start.3 = (f32[4,12,8,128]{3,2,1,0:T(8,128)S(1)}, f32[4,12,8,128]{3,2,1,0:T(8,128)S(1)}, u32[]{:S(2)}, u32[]{:S(2)}) collective-permute-start(f32[4,12,8,128]{3,2,1,0:T(8,128)S(1)} %get-tuple-element.37), channel_id=1, source_target_pairs={{1,2},{2,1},{3,4},{4,3},{5,6},{6,5},{7,8},{8,7},{9,10},{10,9},{11,... | collective-permute-start | bytes 589832 | tf_op jit(solution)/shard_map/ppermute | solution.py:333
  19.6 0.1 collective-permute-start.2
  19.7 4.4 %collective-permute-done.3.refs_5_ = f32[4,12,8,128]{3,2,1,0:T(8,128)S(1)} collective-permute-done((f32[4,12,8,128]{3,2,1,0:T(8,128)S(1)}, f32[4,12,8,128]{3,2,1,0:T(8,128)S(1)}, u32[]{:S(2)}, u32[]{:S(2)}) %collective-permute-start.3) | collective-permute-done | bytes 196640 | tf_op jit(solution)/shard_map/ppermute | solution.py:333
  24.1 26.5 %predict_pass.1.refs_1_ = f32[4,12,8,128]{3,2,1,0:T(8,128)S(1)} custom-call(f32[4,12,8,128]{3,2,1,0:T(8,128)S(1)} %fusion.8.refs_0_.refs_1_, f32[4,12,8,128]{3,2,1,0:T(8,128)S(1)} %fusion.8.refs_0_.refs_1_, f32[2,12,8,128]{3,2,1,0:T(8,128)S(1)} %collective-permute-done.refs_2_, f32[2,12,8,128]{3,2,1,0:T(8,128)S(1)} %collective-permute-done.1.refs_3_, ...), custom_call_target="tpu_custom_call" | custom-call | tf_op jit(solution)/shard_map/predict_pass/pallas_call | solution.py:352
  50.7 4.1 %collective-permute-start.5 = (f32[2,12,8,128]{3,2,1,0:T(8,128)S(1)}, f32[2,12,8,128]{3,2,1,0:T(8,128)S(1)}, u32[]{:S(2)}, u32[]{:S(2)}) collective-permute-start(f32[2,12,8,128]{3,2,1,0:T(8,128)S(1)} %get-tuple-element.45), channel_id=1, source_target_pairs={{16,32},{32,16},{48,64},{64,48},{80,96},{96,80},{17,33},{33,17},{4... | collective-permute-start | bytes 294920 | tf_op jit(solution)/shard_map/ppermute | solution.py:333
  54.8 2.3 %collective-permute-start.4 = (f32[2,12,8,128]{3,2,1,0:T(8,128)S(1)}, f32[2,12,8,128]{3,2,1,0:T(8,128)S(1)}, u32[]{:S(2)}, u32[]{:S(2)}) collective-permute-start(f32[2,12,8,128]{3,2,1,0:T(8,128)S(1)} %get-tuple-element.46), channel_id=1, source_target_pairs={{0,16},{16,0},{32,48},{48,32},{64,80},{80,64},{96,112},{112,96},{1... | collective-permute-start | bytes 294920 | tf_op jit(solution)/shard_map/ppermute | solution.py:333
  57.2 2.4 %collective-permute-done.5.refs_3_ = f32[2,12,8,128]{3,2,1,0:T(8,128)S(1)} collective-permute-done((f32[2,12,8,128]{3,2,1,0:T(8,128)S(1)}, f32[2,12,8,128]{3,2,1,0:T(8,128)S(1)}, u32[]{:S(2)}, u32[]{:S(2)}) %collective-permute-start.5) | collective-permute-done | bytes 98336 | tf_op jit(solution)/shard_map/ppermute | solution.py:333
  59.6 1.4 %collective-permute-done.4.refs_2_ = f32[2,12,8,128]{3,2,1,0:T(8,128)S(1)} collective-permute-done((f32[2,12,8,128]{3,2,1,0:T(8,128)S(1)}, f32[2,12,8,128]{3,2,1,0:T(8,128)S(1)}, u32[]{:S(2)}, u32[]{:S(2)}) %collective-permute-start.4) | collective-permute-done | bytes 98336 | tf_op jit(solution)/shard_map/ppermute | solution.py:333
  61.1 5.2 %collective-permute-start.7 = (f32[4,12,8,128]{3,2,1,0:T(8,128)S(1)}, f32[4,12,8,128]{3,2,1,0:T(8,128)S(1)}, u32[]{:S(2)}, u32[]{:S(2)}) collective-permute-start(f32[4,12,8,128]{3,2,1,0:T(8,128)S(1)} %get-tuple-element.35), channel_id=1, source_target_pairs={{1,2},{2,1},{3,4},{4,3},{5,6},{6,5},{7,8},{8,7},{9,10},{10,9},{11,... | collective-permute-start | bytes 589832 | tf_op jit(solution)/shard_map/ppermute | solution.py:333
  66.3 0.3 collective-permute-start.6
  66.5 3.6 %collective-permute-done.7.refs_5_ = f32[4,12,8,128]{3,2,1,0:T(8,128)S(1)} collective-permute-done((f32[4,12,8,128]{3,2,1,0:T(8,128)S(1)}, f32[4,12,8,128]{3,2,1,0:T(8,128)S(1)}, u32[]{:S(2)}, u32[]{:S(2)}) %collective-permute-start.7) | collective-permute-done | bytes 196640 | tf_op jit(solution)/shard_map/ppermute | solution.py:333
  70.2 26.5 %correct_pass.1 = f32[4,12,8,128]{3,2,1,0:T(8,128)S(1)} custom-call(f32[4,12,8,128]{3,2,1,0:T(8,128)S(1)} %fusion.8.refs_0_.refs_1_, f32[4,12,8,128]{3,2,1,0:T(8,128)S(1)} %predict_pass.1.refs_1_, f32[2,12,8,128]{3,2,1,0:T(8,128)S(1)} %collective-permute-done.4.refs_2_, f32[2,12,8,128]{3,2,1,0:T(8,128)S(1)} %collective-permute-done.5.refs_3_, ...), custom_call_target="tpu_custom_call" | custom-call | tf_op jit(solution)/shard_map/correct_pass/pallas_call | solution.py:352
  96.8 0.1 reshape.233
  96.9 0.5 copy.28
  97.4 0.5 copy.30
  97.9 0.7 gather_fusion
  98.6 0.7 gather_fusion.1
  99.3 0.1 bitcast_select_fusion.1
  99.4 2.3 %collective-permute-start.8 = (f32[7,192]{0,1:T(8,128)S(1)}, f32[7,192]{0,1:T(8,128)S(1)}, u32[]{:S(2)}, u32[]{:S(2)}) collective-permute-start(f32[7,192]{0,1:T(8,128)S(1)} %get-tuple-element.39), channel_id=1, source_target_pairs={{0,16},{16,0},{32,48},{48,32},{64,80},{80,64},{96,112},{112,96},{1... | collective-permute-start | bytes 16136 | tf_op jit(solution)/shard_map/ppermute | solution.py:333
  101.8 1.9 %collective-permute-start.9 = (f32[7,192]{0,1:T(8,128)S(1)}, f32[7,192]{0,1:T(8,128)S(1)}, u32[]{:S(2)}, u32[]{:S(2)}) collective-permute-start(f32[7,192]{0,1:T(8,128)S(1)} %get-tuple-element.40), channel_id=1, source_target_pairs={{16,32},{32,16},{48,64},{64,48},{80,96},{96,80},{17,33},{33,17},{4... | collective-permute-start | bytes 16136 | tf_op jit(solution)/shard_map/ppermute | solution.py:333
  103.7 0.8 broadcast_select_fusion
  104.4 1.2 %collective-permute-done.8 = f32[7,192]{0,1:T(8,128)S(1)} collective-permute-done((f32[7,192]{0,1:T(8,128)S(1)}, f32[7,192]{0,1:T(8,128)S(1)}, u32[]{:S(2)}, u32[]{:S(2)}) %collective-permute-start.8) | collective-permute-done | bytes 5408 | tf_op jit(solution)/shard_map/ppermute | solution.py:333
  105.6 5.0 %collective-permute-done.9 = f32[7,192]{0,1:T(8,128)S(1)} collective-permute-done((f32[7,192]{0,1:T(8,128)S(1)}, f32[7,192]{0,1:T(8,128)S(1)}, u32[]{:S(2)}, u32[]{:S(2)}) %collective-permute-start.9) | collective-permute-done | bytes 5408 | tf_op jit(solution)/shard_map/ppermute | solution.py:333
  110.7 0.1 copy.32
  110.8 0.6 pad_maximum_fusion.2
  (36 shorter events, 0.9 us)
Async XLA Ops:
  0.6 9.7 %copy-start = (s32[2,1,2,48]{3,2,1,0:T(2,128)S(1)}, s32[2,1,2,48]{3,2,1,0:T(2,128)}, u32[]{:S(2)}) copy-start(s32[2,1,2,48]{3,2,1,0:T(2,128)} %param.11) | copy-start | bytes 2308
  3.9 9.0 %collective-permute-start.1 = (f32[2,12,8,128]{3,2,1,0:T(8,128)S(1)}, f32[2,12,8,128]{3,2,1,0:T(8,128)S(1)}, u32[]{:S(2)}, u32[]{:S(2)}) collective-permute-start(f32[2,12,8,128]{3,2,1,0:T(8,128)S(1)} %get-tuple-element.49), channel_id=1, source_target_pairs={{16,32},{32,16},{48,64},{64,48},{80,96},{96,80},{17,33},{33,17},{4... | collective-permute-start | bytes 294920 | tf_op jit(solution)/shard_map/ppermute | solution.py:333
  8.1 6.8 %collective-permute-start = (f32[2,12,8,128]{3,2,1,0:T(8,128)S(1)}, f32[2,12,8,128]{3,2,1,0:T(8,128)S(1)}, u32[]{:S(2)}, u32[]{:S(2)}) collective-permute-start(f32[2,12,8,128]{3,2,1,0:T(8,128)S(1)} %get-tuple-element.50), channel_id=1, source_target_pairs={{0,16},{16,0},{32,48},{48,32},{64,80},{80,64},{96,112},{112,96},{1... | collective-permute-start | bytes 294920 | tf_op jit(solution)/shard_map/ppermute | solution.py:333
  15.0 9.1 %collective-permute-start.3 = (f32[4,12,8,128]{3,2,1,0:T(8,128)S(1)}, f32[4,12,8,128]{3,2,1,0:T(8,128)S(1)}, u32[]{:S(2)}, u32[]{:S(2)}) collective-permute-start(f32[4,12,8,128]{3,2,1,0:T(8,128)S(1)} %get-tuple-element.37), channel_id=1, source_target_pairs={{1,2},{2,1},{3,4},{4,3},{5,6},{6,5},{7,8},{8,7},{9,10},{10,9},{11,... | collective-permute-start | bytes 589832 | tf_op jit(solution)/shard_map/ppermute | solution.py:333
  19.6 4.5 %collective-permute-start.2 = (f32[4,12,8,128]{3,2,1,0:T(8,128)S(1)}, f32[4,12,8,128]{3,2,1,0:T(8,128)S(1)}, u32[]{:S(2)}, u32[]{:S(2)}) collective-permute-start(f32[4,12,8,128]{3,2,1,0:T(8,128)S(1)} %get-tuple-element.38), channel_id=1, source_target_pairs={{0,1},{1,0},{2,3},{3,2},{4,5},{5,4},{6,7},{7,6},{8,9},{9,8},{10,11... | collective-permute-start | bytes 589832 | tf_op jit(solution)/shard_map/ppermute | solution.py:333
  50.7 8.9 %collective-permute-start.5 = (f32[2,12,8,128]{3,2,1,0:T(8,128)S(1)}, f32[2,12,8,128]{3,2,1,0:T(8,128)S(1)}, u32[]{:S(2)}, u32[]{:S(2)}) collective-permute-start(f32[2,12,8,128]{3,2,1,0:T(8,128)S(1)} %get-tuple-element.45), channel_id=1, source_target_pairs={{16,32},{32,16},{48,64},{64,48},{80,96},{96,80},{17,33},{33,17},{4... | collective-permute-start | bytes 294920 | tf_op jit(solution)/shard_map/ppermute | solution.py:333
  54.8 6.2 %collective-permute-start.4 = (f32[2,12,8,128]{3,2,1,0:T(8,128)S(1)}, f32[2,12,8,128]{3,2,1,0:T(8,128)S(1)}, u32[]{:S(2)}, u32[]{:S(2)}) collective-permute-start(f32[2,12,8,128]{3,2,1,0:T(8,128)S(1)} %get-tuple-element.46), channel_id=1, source_target_pairs={{0,16},{16,0},{32,48},{48,32},{64,80},{80,64},{96,112},{112,96},{1... | collective-permute-start | bytes 294920 | tf_op jit(solution)/shard_map/ppermute | solution.py:333
  61.1 9.1 %collective-permute-start.7 = (f32[4,12,8,128]{3,2,1,0:T(8,128)S(1)}, f32[4,12,8,128]{3,2,1,0:T(8,128)S(1)}, u32[]{:S(2)}, u32[]{:S(2)}) collective-permute-start(f32[4,12,8,128]{3,2,1,0:T(8,128)S(1)} %get-tuple-element.35), channel_id=1, source_target_pairs={{1,2},{2,1},{3,4},{4,3},{5,6},{6,5},{7,8},{8,7},{9,10},{10,9},{11,... | collective-permute-start | bytes 589832 | tf_op jit(solution)/shard_map/ppermute | solution.py:333
  66.3 3.9 %collective-permute-start.6 = (f32[4,12,8,128]{3,2,1,0:T(8,128)S(1)}, f32[4,12,8,128]{3,2,1,0:T(8,128)S(1)}, u32[]{:S(2)}, u32[]{:S(2)}) collective-permute-start(f32[4,12,8,128]{3,2,1,0:T(8,128)S(1)} %get-tuple-element.36), channel_id=1, source_target_pairs={{0,1},{1,0},{2,3},{3,2},{4,5},{5,4},{6,7},{7,6},{8,9},{9,8},{10,11... | collective-permute-start | bytes 589832 | tf_op jit(solution)/shard_map/ppermute | solution.py:333
  99.4 6.2 %collective-permute-start.8 = (f32[7,192]{0,1:T(8,128)S(1)}, f32[7,192]{0,1:T(8,128)S(1)}, u32[]{:S(2)}, u32[]{:S(2)}) collective-permute-start(f32[7,192]{0,1:T(8,128)S(1)} %get-tuple-element.39), channel_id=1, source_target_pairs={{0,16},{16,0},{32,48},{48,32},{64,80},{80,64},{96,112},{112,96},{1... | collective-permute-start | bytes 16136 | tf_op jit(solution)/shard_map/ppermute | solution.py:333
  101.8 8.9 %collective-permute-start.9 = (f32[7,192]{0,1:T(8,128)S(1)}, f32[7,192]{0,1:T(8,128)S(1)}, u32[]{:S(2)}, u32[]{:S(2)}) collective-permute-start(f32[7,192]{0,1:T(8,128)S(1)} %get-tuple-element.40), channel_id=1, source_target_pairs={{16,32},{32,16},{48,64},{64,48},{80,96},{96,80},{17,33},{33,17},{4... | collective-permute-start | bytes 16136 | tf_op jit(solution)/shard_map/ppermute | solution.py:333

commit v5 on v4

--- a/solution.py
+++ b/solution.py
@@ -9,6 +9,7 @@
 
 SLOTS = 32
 LMAX = 4
+FACE_ROWS = 192
 CZ = 48
 BLOCKS = 12
 
@@ -269,8 +270,23 @@
     reduce(4 * BLOCKS - 1, 3)
 
 
-def pass_kernel(final, base, own, slab_a, slab_b, tile_a, tile_b, out,
+def leaving(fields, x, source):
+    number = lax.broadcasted_iota(jnp.int32, (256, 256), 0)
+    source = jnp.broadcast_to(source[0:1], (256, 256))
+    total = jnp.zeros((32, 256), jnp.float32)
+    for y in range(2):
+        for h in range(6):
+            vals = jnp.concatenate([fields[2 * x + y, 2 * h], fields[2 * x + y, 2 * h + 1]], axis=1)
+            rows = jnp.concatenate([*pieces(vals), jnp.zeros((8, 256), jnp.float32)], axis=0)
+            hit = jnp.where(number == source - 256 * (6 * y + h), 1.0, 0.0)
+            total = total + jnp.dot(rows.astype(jnp.bfloat16), hit.astype(jnp.bfloat16),
+                                    preferred_element_type=jnp.float32)
+    return (total[0:8] + total[8:16] + total[16:24])[:7, :FACE_ROWS]
+
+
+def pass_kernel(final, base, own, slab_a, slab_b, tile_a, tile_b, sources, outs,
                 cols, blocks, lhs, places, res, forces, drifts, *bufs):
+    out = outs[0]
     center_blocks(own, blocks)
     odd_s = lax.axis_index("slab") % 2
     odd_t = lax.axis_index("tile") % 2
@@ -323,6 +339,13 @@
         swap_back(lambda r: res[c, r], store)
         return 0
     lax.fori_loop(0, 4, finish, 0)
+    for k in range(2):
+        x = (1 - odd_s + k) % 2
+        if final:
+            outs[1 + k][...] = leaving(out, x, sources[0][x])
+        else:
+            for y in range(2):
+                outs[1 + k][y] = out[2 * x + y]
 
 
 def swapped(value, axis, first):
@@ -333,12 +356,10 @@
     return lax.ppermute(value, axis, trades)
 
 
-def rates_pass(final, base, own):
-    odd_s = lax.axis_index("slab") % 2
+def rates_pass(final, base, own, faces, extra=()):
     odd_t = lax.axis_index("tile") % 2
     grid = own.reshape(2, 2, BLOCKS, 8, 128)
-    slabs = [swapped(lax.dynamic_index_in_dim(grid, (1 - odd_s + k) % 2, 0, False), "slab", k)
-             for k in range(2)]
+    slabs = [swapped(faces[k], "slab", k) for k in range(2)]
 
     def edge(k):
         at = (1 - odd_t + k) % 2
@@ -346,12 +367,16 @@
         return lax.dynamic_index_in_dim(four, at, 1, False)
     tiles = [swapped(edge(k), "tile", k) for k in range(2)]
 
+    ins = 6 + len(extra)
+
     def body(*refs):
-        pass_kernel(final, *refs)
+        pass_kernel(final, *refs[:6], refs[6:ins], refs[ins:ins + 3], *refs[ins + 3:])
+    whole = jax.ShapeDtypeStruct((4, BLOCKS, 8, 128), jnp.float32)
+    face = jax.ShapeDtypeStruct((7, FACE_ROWS) if final else (2, BLOCKS, 8, 128), jnp.float32)
     work = [pltpu.VMEM((256, 512), jnp.bfloat16), pltpu.VMEM((864, 512), jnp.float32)]
     return pl.pallas_call(
         body,
-        out_shape=jax.ShapeDtypeStruct((4, BLOCKS, 8, 128), jnp.float32),
+        out_shape=(whole, face, face),
         scratch_shapes=[pltpu.VMEM((16, BLOCKS, 8, 128), jnp.float32),
                         pltpu.VMEM((4, BLOCKS, 8, 128), jnp.float32),
                         pltpu.VMEM((16, SPAN, 256), jnp.bfloat16),
@@ -362,7 +387,7 @@
                         *work, *work],
         compiler_params=pltpu.CompilerParams(vmem_limit_bytes=40 << 20),
         name="correct_pass" if final else "predict_pass",
-    )(base, own, *slabs, *tiles)
+    )(base, own, *slabs, *tiles, *extra)
 
 
 def slot_mask(cell_counts):
@@ -370,19 +395,17 @@
     return slot < cell_counts[..., None]
 
 
-def pack_leavers(face_state, face_count, face_leave):
+def leaver_sources(face_count, face_leave):
     cell_total = face_count.shape[0] * face_count.shape[1]
-    row_total = cell_total * LMAX // 2
     leave_quota = face_leave.reshape(cell_total)
     occupancy = face_count.reshape(cell_total)
     row_ends = jnp.cumsum(leave_quota, dtype=jnp.int32)
     starts = row_ends - leave_quota
-    row_ids = jnp.arange(row_total, dtype=jnp.int32)
+    row_ids = jnp.arange(FACE_ROWS, dtype=jnp.int32)
     owner_mask = (starts[None, :] <= row_ids[:, None]) & (row_ends[None, :] > row_ids[:, None])
     root = jnp.arange(cell_total, dtype=jnp.int32) * SLOTS + occupancy - leave_quota - starts
     source_row = jnp.sum(jnp.where(owner_mask, root[None, :], 0), axis=1, dtype=jnp.int32) + row_ids
-    flat_face = face_state.reshape(7, cell_total * SLOTS)
-    return jnp.take(flat_face, source_row, axis=1)
+    return jnp.pad(source_row, (0, 256 - FACE_ROWS), constant_values=-1)
 
 
 def start_fields(particles, counts):
@@ -400,15 +423,18 @@
 
 def shards(particles, counts, leavers):
     fields = start_fields(particles, counts)
-    middle = rates_pass(False, fields, fields)
-    updated = finish_fields(rates_pass(True, fields, middle))
+    odd = lax.axis_index("slab") % 2
+    grid = fields.reshape(2, 2, BLOCKS, 8, 128)
+    faces = [lax.dynamic_index_in_dim(grid, (1 - odd + k) % 2, 0, False) for k in range(2)]
+    middle, *faces = rates_pass(False, fields, fields, faces)
+    sources = jnp.stack([leaver_sources(counts[k], leavers[k, 0]) for k in range(2)])
+    sources = jnp.broadcast_to(sources[:, None], (2, 8, 256))
+    updated, *rows = rates_pass(True, fields, middle, faces, (sources,))
+    updated = finish_fields(updated)
     remain = counts.at[0].add(-leavers[0, 0]).at[1].add(-leavers[1, 0])
     kept = jnp.where(slot_mask(remain).reshape(1, 2, 2, CZ * SLOTS), updated, 0.0)
-    lower_rows = pack_leavers(updated[:, 0], counts[0], leavers[0, 0])
-    upper_rows = pack_leavers(updated[:, 1], counts[1], leavers[1, 0])
-    odd = lax.axis_index("slab") % 2 == 1
-    first = swapped(jnp.where(odd, lower_rows, upper_rows), "slab", 0)
-    second = swapped(jnp.where(odd, upper_rows, lower_rows), "slab", 1)
+    first, second = swapped(rows[0], "slab", 0), swapped(rows[1], "slab", 1)
+    odd = odd == 1
     return (kept, jnp.stack([jnp.where(odd, first, second), jnp.where(odd, second, first)]))
 
 

time: 112 us -> 108 us (0.964)
  starting transfers between devices: 27.2 us -> 25.5 us
  local copies, waits for them, and re-layouts: 5.93 us -> 4.27 us
  other arithmetic: 3.3 us -> 1.79 us
    unnamed x3 -> x6, local copies, waits for them, and re-layouts: 0.69 us -> 2.55 us
    ppermute x10, starting transfers between devices: 27.2 us -> 25.5 us  [swapped(): return lax.ppermute(value, axis, trades)]
    gather x2 -> x0, local copies, waits for them, and re-layouts: 1.4 us -> none  [pack_leavers(): return jnp.take(flat_face, source_row, axis=1)]
where the time goes in v5:
time: 108 us
  Pallas kernels  53.7 us (50%)
  starting transfers between devices  25.5 us (24%)
  waiting for transfers between devices  21.5 us (20%)
  local copies, waits for them, and re-layouts  4.27 us (4%)
  other arithmetic  1.79 us (2%)
    pallas_call x2, Pallas kernels, rates_pass(): pl.pallas_call(body, out_shape=(whole, face, face), scratch_shapes=[pltpu...  53.7 us
    ppermute x10, starting transfers between devices, swapped(): return lax.ppermute(value, axis, trades)  25.5 us
    ppermute x10, waiting for transfers between devices, swapped(): return lax.ppermute(value, axis, trades)  21.5 us
    unnamed x6, local copies, waits for them, and re-layouts  2.55 us
  transfers between devices with their start and end apart: 10, of which 8 were waited for; matrix products, arithmetic and copies ran while one was open for 2% of the time, Pallas kernels for 0%

profile of v5, /device:TPU:10, one launch (start us, length us, event | category | flops | bytes accessed | tf_op | source)
XLA Modules:
  0.0 107.7 jit_solution(15830960824109503509)
XLA Ops:
  0.6 0.7 copy.21
  1.3 0.1 lt.89
  1.4 0.1 lt.92
  1.5 0.1 lt.90
  1.6 0.1 iota.49
  1.7 0.6 copy-done
  2.3 0.1 concatenate.12
  2.6 0.1 iota.52
  2.6 0.1 copy.13
  2.8 0.1 maximum_select_fusion
  2.9 4.2 %collective-permute-start.1 = (f32[2,12,8,128]{3,2,1,0:T(8,128)S(1)}, f32[2,12,8,128]{3,2,1,0:T(8,128)S(1)}, u32[]{:S(2)}, u32[]{:S(2)}) collective-permute-start(f32[2,12,8,128]{3,2,1,0:T(8,128)S(1)} %get-tuple-element.56), channel_id=1, source_target_pairs={{16,32},{32,16},{48,64},{64,48},{80,96},{96,80},{17,33},{33,17},{4... | collective-permute-start | bytes 294920 | tf_op jit(solution)/shard_map/ppermute | solution.py:356
  7.1 2.3 %collective-permute-start = (f32[2,12,8,128]{3,2,1,0:T(8,128)S(1)}, f32[2,12,8,128]{3,2,1,0:T(8,128)S(1)}, u32[]{:S(2)}, u32[]{:S(2)}) collective-permute-start(f32[2,12,8,128]{3,2,1,0:T(8,128)S(1)} %get-tuple-element.57), channel_id=1, source_target_pairs={{0,16},{16,0},{32,48},{48,32},{64,80},{80,64},{96,112},{112,96},{1... | collective-permute-start | bytes 294920 | tf_op jit(solution)/shard_map/ppermute | solution.py:356
  9.4 0.6 copy-done.1
  10.0 0.1 reshape.232
  10.2 0.1 reshape_squeeze.12
  10.2 0.1 reshape.233
  10.4 0.1 reshape_squeeze.14
  10.5 0.1 reduce-window.14
  10.6 0.1 reduce.4
  10.7 0.1 reshape_squeeze.13
  10.8 0.1 reduce-window.15
  10.9 0.1 reduce.5
  11.0 0.1 reshape_squeeze.15
  11.1 0.1 lt.86
  11.2 0.1 lt.87
  11.4 0.1 select_reduce_fusion.1
  11.5 0.1 select_reduce_fusion
  11.7 0.2 collective-permute-done.1.refs_3_
  11.9 2.0 %collective-permute-done.refs_2_ = f32[2,12,8,128]{3,2,1,0:T(8,128)S(1)} collective-permute-done((f32[2,12,8,128]{3,2,1,0:T(8,128)S(1)}, f32[2,12,8,128]{3,2,1,0:T(8,128)S(1)}, u32[]{:S(2)}, u32[]{:S(2)}) %collective-permute-start) | collective-permute-done | bytes 98336 | tf_op jit(solution)/shard_map/ppermute | solution.py:356
  14.0 0.1 collective-permute-start.2
  14.1 6.2 %collective-permute-start.3 = (f32[4,12,8,128]{3,2,1,0:T(8,128)S(1)}, f32[4,12,8,128]{3,2,1,0:T(8,128)S(1)}, u32[]{:S(2)}, u32[]{:S(2)}) collective-permute-start(f32[4,12,8,128]{3,2,1,0:T(8,128)S(1)} %get-tuple-element.50), channel_id=1, source_target_pairs={{1,2},{2,1},{3,4},{4,3},{5,6},{6,5},{7,8},{8,7},{9,10},{10,9},{11,... | collective-permute-start | bytes 589832 | tf_op jit(solution)/shard_map/ppermute | solution.py:356
  20.3 3.3 %collective-permute-done.3.refs_5_ = f32[4,12,8,128]{3,2,1,0:T(8,128)S(1)} collective-permute-done((f32[4,12,8,128]{3,2,1,0:T(8,128)S(1)}, f32[4,12,8,128]{3,2,1,0:T(8,128)S(1)}, u32[]{:S(2)}, u32[]{:S(2)}) %collective-permute-start.3) | collective-permute-done | bytes 196640 | tf_op jit(solution)/shard_map/ppermute | solution.py:356
  23.6 26.5 %predict_pass.1 = (f32[4,12,8,128]{3,2,1,0:T(8,128)S(1)}, f32[2,12,8,128]{3,2,1,0:T(8,128)S(1)}, f32[2,12,8,128]{3,2,1,0:T(8,128)S(1)}) custom-call(f32[4,12,8,128]{3,2,1,0:T(8,128)S(1)} %fusion.6.refs_0_.refs_1_, f32[4,12,8,128]{3,2,1,0:T(8,128)S(1)} %fusion.6.refs_0_.refs_1_, f32[2,12,8,128]{3,2,1,0:T(8,128)S(1)} %collective-permute-done.refs_2_, ...), custom_call_target="tpu_custom_call" | custom-call | tf_op jit(solution)/shard_map/predict_pass/pallas_call | solution.py:377
  50.2 2.3 %collective-permute-start.4 = (f32[2,12,8,128]{3,2,1,0:T(8,128)S(1)}, f32[2,12,8,128]{3,2,1,0:T(8,128)S(1)}, u32[]{:S(2)}, u32[]{:S(2)}) collective-permute-start(f32[2,12,8,128]{3,2,1,0:T(8,128)S(1)} %get-tuple-element.33), channel_id=1, source_target_pairs={{0,16},{16,0},{32,48},{48,32},{64,80},{80,64},{96,112},{112,96},{1... | collective-permute-start | bytes 294920 | tf_op jit(solution)/shard_map/ppermute | solution.py:356
  52.5 2.0 %collective-permute-start.5 = (f32[2,12,8,128]{3,2,1,0:T(8,128)S(1)}, f32[2,12,8,128]{3,2,1,0:T(8,128)S(1)}, u32[]{:S(2)}, u32[]{:S(2)}) collective-permute-start(f32[2,12,8,128]{3,2,1,0:T(8,128)S(1)} %get-tuple-element.34), channel_id=1, source_target_pairs={{16,32},{32,16},{48,64},{64,48},{80,96},{96,80},{17,33},{33,17},{4... | collective-permute-start | bytes 294920 | tf_op jit(solution)/shard_map/ppermute | solution.py:356
  54.5 1.8 %collective-permute-done.4.refs_2_ = f32[2,12,8,128]{3,2,1,0:T(8,128)S(1)} collective-permute-done((f32[2,12,8,128]{3,2,1,0:T(8,128)S(1)}, f32[2,12,8,128]{3,2,1,0:T(8,128)S(1)}, u32[]{:S(2)}, u32[]{:S(2)}) %collective-permute-start.4) | collective-permute-done | bytes 98336 | tf_op jit(solution)/shard_map/ppermute | solution.py:356
  56.4 5.0 %collective-permute-done.5.refs_3_ = f32[2,12,8,128]{3,2,1,0:T(8,128)S(1)} collective-permute-done((f32[2,12,8,128]{3,2,1,0:T(8,128)S(1)}, f32[2,12,8,128]{3,2,1,0:T(8,128)S(1)}, u32[]{:S(2)}, u32[]{:S(2)}) %collective-permute-start.5) | collective-permute-done | bytes 98336 | tf_op jit(solution)/shard_map/ppermute | solution.py:356
  61.4 0.1 collective-permute-start.6
  61.5 5.1 %collective-permute-start.7 = (f32[4,12,8,128]{3,2,1,0:T(8,128)S(1)}, f32[4,12,8,128]{3,2,1,0:T(8,128)S(1)}, u32[]{:S(2)}, u32[]{:S(2)}) collective-permute-start(f32[4,12,8,128]{3,2,1,0:T(8,128)S(1)} %get-tuple-element.48), channel_id=1, source_target_pairs={{1,2},{2,1},{3,4},{4,3},{5,6},{6,5},{7,8},{8,7},{9,10},{10,9},{11,... | collective-permute-start | bytes 589832 | tf_op jit(solution)/shard_map/ppermute | solution.py:356
  66.7 3.9 %collective-permute-done.7.refs_5_ = f32[4,12,8,128]{3,2,1,0:T(8,128)S(1)} collective-permute-done((f32[4,12,8,128]{3,2,1,0:T(8,128)S(1)}, f32[4,12,8,128]{3,2,1,0:T(8,128)S(1)}, u32[]{:S(2)}, u32[]{:S(2)}) %collective-permute-start.7) | collective-permute-done | bytes 196640 | tf_op jit(solution)/shard_map/ppermute | solution.py:356
  70.6 27.2 %correct_pass.1 = (f32[4,12,8,128]{3,2,1,0:T(8,128)S(1)}, f32[7,192]{1,0:T(8,128)S(1)}, f32[7,192]{1,0:T(8,128)S(1)}) custom-call(f32[4,12,8,128]{3,2,1,0:T(8,128)S(1)} %fusion.6.refs_0_.refs_1_, f32[4,12,8,128]{3,2,1,0:T(8,128)S(1)} %get-tuple-element.32.refs_1_, f32[2,12,8,128]{3,2,1,0:T(8,128)S(1)} %collective-permute-done.4.refs_2_, ...), custom_call_target="tpu_custom_call" | custom-call | tf_op jit(solution)/shard_map/correct_pass/pallas_call | solution.py:377
  97.8 1.4 %collective-permute-start.8 = (f32[7,192]{1,0:T(8,128)S(1)}, f32[7,192]{1,0:T(8,128)S(1)}, u32[]{:S(2)}, u32[]{:S(2)}) collective-permute-start(f32[7,192]{1,0:T(8,128)S(1)} %get-tuple-element.36), channel_id=1, source_target_pairs={{0,16},{16,0},{32,48},{48,32},{64,80},{80,64},{96,112},{112,96},{1... | collective-permute-start | bytes 16136 | tf_op jit(solution)/shard_map/ppermute | solution.py:356
  99.2 1.9 %collective-permute-start.9 = (f32[7,192]{1,0:T(8,128)S(1)}, f32[7,192]{1,0:T(8,128)S(1)}, u32[]{:S(2)}, u32[]{:S(2)}) collective-permute-start(f32[7,192]{1,0:T(8,128)S(1)} %get-tuple-element.37), channel_id=1, source_target_pairs={{16,32},{32,16},{48,64},{64,48},{80,96},{96,80},{17,33},{33,17},{4... | collective-permute-start | bytes 16136 | tf_op jit(solution)/shard_map/ppermute | solution.py:356
  101.1 0.1 reshape.231
  101.2 0.8 broadcast_select_fusion
  102.0 1.0 collective-permute-done.8
  103.0 4.1 %collective-permute-done.9 = f32[7,192]{1,0:T(8,128)S(1)} collective-permute-done((f32[7,192]{1,0:T(8,128)S(1)}, f32[7,192]{1,0:T(8,128)S(1)}, u32[]{:S(2)}, u32[]{:S(2)}) %collective-permute-start.9) | collective-permute-done | bytes 5408 | tf_op jit(solution)/shard_map/ppermute | solution.py:356
  107.1 0.6 copy.17
  (32 shorter events, 0.5 us)
Async XLA Ops:
  1.4 0.9 copy-start
  2.9 9.0 %collective-permute-start.1 = (f32[2,12,8,128]{3,2,1,0:T(8,128)S(1)}, f32[2,12,8,128]{3,2,1,0:T(8,128)S(1)}, u32[]{:S(2)}, u32[]{:S(2)}) collective-permute-start(f32[2,12,8,128]{3,2,1,0:T(8,128)S(1)} %get-tuple-element.56), channel_id=1, source_target_pairs={{16,32},{32,16},{48,64},{64,48},{80,96},{96,80},{17,33},{33,17},{4... | collective-permute-start | bytes 294920 | tf_op jit(solution)/shard_map/ppermute | solution.py:356
  7.1 6.8 %collective-permute-start = (f32[2,12,8,128]{3,2,1,0:T(8,128)S(1)}, f32[2,12,8,128]{3,2,1,0:T(8,128)S(1)}, u32[]{:S(2)}, u32[]{:S(2)}) collective-permute-start(f32[2,12,8,128]{3,2,1,0:T(8,128)S(1)} %get-tuple-element.57), channel_id=1, source_target_pairs={{0,16},{16,0},{32,48},{48,32},{64,80},{80,64},{96,112},{112,96},{1... | collective-permute-start | bytes 294920 | tf_op jit(solution)/shard_map/ppermute | solution.py:356
  9.3 0.7 copy-start.1
  14.0 6.3 %collective-permute-start.2 = (f32[4,12,8,128]{3,2,1,0:T(8,128)S(1)}, f32[4,12,8,128]{3,2,1,0:T(8,128)S(1)}, u32[]{:S(2)}, u32[]{:S(2)}) collective-permute-start(f32[4,12,8,128]{3,2,1,0:T(8,128)S(1)} %get-tuple-element.51), channel_id=1, source_target_pairs={{0,1},{1,0},{2,3},{3,2},{4,5},{5,4},{6,7},{7,6},{8,9},{9,8},{10,11... | collective-permute-start | bytes 589832 | tf_op jit(solution)/shard_map/ppermute | solution.py:356
  14.1 9.5 %collective-permute-start.3 = (f32[4,12,8,128]{3,2,1,0:T(8,128)S(1)}, f32[4,12,8,128]{3,2,1,0:T(8,128)S(1)}, u32[]{:S(2)}, u32[]{:S(2)}) collective-permute-start(f32[4,12,8,128]{3,2,1,0:T(8,128)S(1)} %get-tuple-element.50), channel_id=1, source_target_pairs={{1,2},{2,1},{3,4},{4,3},{5,6},{6,5},{7,8},{8,7},{9,10},{10,9},{11,... | collective-permute-start | bytes 589832 | tf_op jit(solution)/shard_map/ppermute | solution.py:356
  50.2 6.2 %collective-permute-start.4 = (f32[2,12,8,128]{3,2,1,0:T(8,128)S(1)}, f32[2,12,8,128]{3,2,1,0:T(8,128)S(1)}, u32[]{:S(2)}, u32[]{:S(2)}) collective-permute-start(f32[2,12,8,128]{3,2,1,0:T(8,128)S(1)} %get-tuple-element.33), channel_id=1, source_target_pairs={{0,16},{16,0},{32,48},{48,32},{64,80},{80,64},{96,112},{112,96},{1... | collective-permute-start | bytes 294920 | tf_op jit(solution)/shard_map/ppermute | solution.py:356
  52.5 8.9 %collective-permute-start.5 = (f32[2,12,8,128]{3,2,1,0:T(8,128)S(1)}, f32[2,12,8,128]{3,2,1,0:T(8,128)S(1)}, u32[]{:S(2)}, u32[]{:S(2)}) collective-permute-start(f32[2,12,8,128]{3,2,1,0:T(8,128)S(1)} %get-tuple-element.34), channel_id=1, source_target_pairs={{16,32},{32,16},{48,64},{64,48},{80,96},{96,80},{17,33},{33,17},{4... | collective-permute-start | bytes 294920 | tf_op jit(solution)/shard_map/ppermute | solution.py:356
  61.4 5.3 %collective-permute-start.6 = (f32[4,12,8,128]{3,2,1,0:T(8,128)S(1)}, f32[4,12,8,128]{3,2,1,0:T(8,128)S(1)}, u32[]{:S(2)}, u32[]{:S(2)}) collective-permute-start(f32[4,12,8,128]{3,2,1,0:T(8,128)S(1)} %get-tuple-element.49), channel_id=1, source_target_pairs={{0,1},{1,0},{2,3},{3,2},{4,5},{5,4},{6,7},{7,6},{8,9},{9,8},{10,11... | collective-permute-start | bytes 589832 | tf_op jit(solution)/shard_map/ppermute | solution.py:356
  61.5 9.1 %collective-permute-start.7 = (f32[4,12,8,128]{3,2,1,0:T(8,128)S(1)}, f32[4,12,8,128]{3,2,1,0:T(8,128)S(1)}, u32[]{:S(2)}, u32[]{:S(2)}) collective-permute-start(f32[4,12,8,128]{3,2,1,0:T(8,128)S(1)} %get-tuple-element.48), channel_id=1, source_target_pairs={{1,2},{2,1},{3,4},{4,3},{5,6},{6,5},{7,8},{8,7},{9,10},{10,9},{11,... | collective-permute-start | bytes 589832 | tf_op jit(solution)/shard_map/ppermute | solution.py:356
  97.8 5.2 %collective-permute-start.8 = (f32[7,192]{1,0:T(8,128)S(1)}, f32[7,192]{1,0:T(8,128)S(1)}, u32[]{:S(2)}, u32[]{:S(2)}) collective-permute-start(f32[7,192]{1,0:T(8,128)S(1)} %get-tuple-element.36), channel_id=1, source_target_pairs={{0,16},{16,0},{32,48},{48,32},{64,80},{80,64},{96,112},{112,96},{1... | collective-permute-start | bytes 16136 | tf_op jit(solution)/shard_map/ppermute | solution.py:356
  99.2 7.9 %collective-permute-start.9 = (f32[7,192]{1,0:T(8,128)S(1)}, f32[7,192]{1,0:T(8,128)S(1)}, u32[]{:S(2)}, u32[]{:S(2)}) collective-permute-start(f32[7,192]{1,0:T(8,128)S(1)} %get-tuple-element.37), channel_id=1, source_target_pairs={{16,32},{32,16},{48,64},{64,48},{80,96},{96,80},{17,33},{33,17},{4... | collective-permute-start | bytes 16136 | tf_op jit(solution)/shard_map/ppermute | solution.py:356

commit v6 on v5

--- a/solution.py
+++ b/solution.py
@@ -27,7 +27,7 @@
 visc_gain = 2.0 * viscosity * sound_speed * smoothing
 FAR = 2.0**50
 MIDDLE = 5.5
-UNROLL = 12
+UNROLL = 24
 SPAN = 32 * (BLOCKS + 2)
 AROUND = (0, 1, 2, 4, 5, 6, 8, 9, 10)
 

time: 108 us -> 107 us (level)
  no operation moved by 1% of the time
where the time goes in v6:
time: 107 us
  Pallas kernels  53 us (50%)
  starting transfers between devices  25.8 us (24%)
  waiting for transfers between devices  21.2 us (20%)
  local copies, waits for them, and re-layouts  4.27 us (4%)
  other arithmetic  1.79 us (2%)
    pallas_call x2, Pallas kernels, rates_pass(): pl.pallas_call(body, out_shape=(whole, face, face), scratch_shapes=[pltpu...  53 us
    ppermute x10, starting transfers between devices, swapped(): return lax.ppermute(value, axis, trades)  25.8 us
    ppermute x10, waiting for transfers between devices, swapped(): return lax.ppermute(value, axis, trades)  21.2 us
    unnamed x6, local copies, waits for them, and re-layouts  2.55 us
  transfers between devices with their start and end apart: 10, of which 8 were waited for; matrix products, arithmetic and copies ran while one was open for 2% of the time, Pallas kernels for 0%

profile of v6, /device:TPU:10, one launch (start us, length us, event | category | flops | bytes accessed | tf_op | source)
XLA Modules:
  0.0 107.0 jit_solution(3645395058573803550)
XLA Ops:
  0.6 0.7 copy.21
  1.3 0.1 lt.89
  1.4 0.1 lt.92
  1.5 0.1 lt.90
  1.6 0.1 iota.49
  1.7 0.6 copy-done
  2.3 0.1 concatenate.12
  2.6 0.1 iota.52
  2.6 0.1 copy.13
  2.8 0.1 maximum_select_fusion
  2.9 4.2 %collective-permute-start.1 = (f32[2,12,8,128]{3,2,1,0:T(8,128)S(1)}, f32[2,12,8,128]{3,2,1,0:T(8,128)S(1)}, u32[]{:S(2)}, u32[]{:S(2)}) collective-permute-start(f32[2,12,8,128]{3,2,1,0:T(8,128)S(1)} %get-tuple-element.56), channel_id=1, source_target_pairs={{16,32},{32,16},{48,64},{64,48},{80,96},{96,80},{17,33},{33,17},{4... | collective-permute-start | bytes 294920 | tf_op jit(solution)/shard_map/ppermute | solution.py:356
  7.1 2.3 %collective-permute-start = (f32[2,12,8,128]{3,2,1,0:T(8,128)S(1)}, f32[2,12,8,128]{3,2,1,0:T(8,128)S(1)}, u32[]{:S(2)}, u32[]{:S(2)}) collective-permute-start(f32[2,12,8,128]{3,2,1,0:T(8,128)S(1)} %get-tuple-element.57), channel_id=1, source_target_pairs={{0,16},{16,0},{32,48},{48,32},{64,80},{80,64},{96,112},{112,96},{1... | collective-permute-start | bytes 294920 | tf_op jit(solution)/shard_map/ppermute | solution.py:356
  9.4 0.6 copy-done.1
  10.0 0.1 reshape.232
  10.2 0.1 reshape_squeeze.12
  10.2 0.1 reshape.233
  10.4 0.1 reshape_squeeze.14
  10.5 0.1 reduce-window.14
  10.6 0.1 reduce.4
  10.7 0.1 reshape_squeeze.13
  10.8 0.1 reduce-window.15
  10.9 0.1 reduce.5
  11.0 0.1 reshape_squeeze.15
  11.1 0.1 lt.86
  11.2 0.1 lt.87
  11.4 0.1 select_reduce_fusion.1
  11.5 0.1 select_reduce_fusion
  11.7 0.2 collective-permute-done.1.refs_3_
  11.9 2.0 %collective-permute-done.refs_2_ = f32[2,12,8,128]{3,2,1,0:T(8,128)S(1)} collective-permute-done((f32[2,12,8,128]{3,2,1,0:T(8,128)S(1)}, f32[2,12,8,128]{3,2,1,0:T(8,128)S(1)}, u32[]{:S(2)}, u32[]{:S(2)}) %collective-permute-start) | collective-permute-done | bytes 98336 | tf_op jit(solution)/shard_map/ppermute | solution.py:356
  14.0 0.1 collective-permute-start.2
  14.1 6.4 %collective-permute-start.3 = (f32[4,12,8,128]{3,2,1,0:T(8,128)S(1)}, f32[4,12,8,128]{3,2,1,0:T(8,128)S(1)}, u32[]{:S(2)}, u32[]{:S(2)}) collective-permute-start(f32[4,12,8,128]{3,2,1,0:T(8,128)S(1)} %get-tuple-element.50), channel_id=1, source_target_pairs={{1,2},{2,1},{3,4},{4,3},{5,6},{6,5},{7,8},{8,7},{9,10},{10,9},{11,... | collective-permute-start | bytes 589832 | tf_op jit(solution)/shard_map/ppermute | solution.py:356
  20.5 3.1 %collective-permute-done.3.refs_5_ = f32[4,12,8,128]{3,2,1,0:T(8,128)S(1)} collective-permute-done((f32[4,12,8,128]{3,2,1,0:T(8,128)S(1)}, f32[4,12,8,128]{3,2,1,0:T(8,128)S(1)}, u32[]{:S(2)}, u32[]{:S(2)}) %collective-permute-start.3) | collective-permute-done | bytes 196640 | tf_op jit(solution)/shard_map/ppermute | solution.py:356
  23.6 26.2 %predict_pass.1 = (f32[4,12,8,128]{3,2,1,0:T(8,128)S(1)}, f32[2,12,8,128]{3,2,1,0:T(8,128)S(1)}, f32[2,12,8,128]{3,2,1,0:T(8,128)S(1)}) custom-call(f32[4,12,8,128]{3,2,1,0:T(8,128)S(1)} %fusion.6.refs_0_.refs_1_, f32[4,12,8,128]{3,2,1,0:T(8,128)S(1)} %fusion.6.refs_0_.refs_1_, f32[2,12,8,128]{3,2,1,0:T(8,128)S(1)} %collective-permute-done.refs_2_, ...), custom_call_target="tpu_custom_call" | custom-call | tf_op jit(solution)/shard_map/predict_pass/pallas_call | solution.py:377
  49.8 2.3 %collective-permute-start.4 = (f32[2,12,8,128]{3,2,1,0:T(8,128)S(1)}, f32[2,12,8,128]{3,2,1,0:T(8,128)S(1)}, u32[]{:S(2)}, u32[]{:S(2)}) collective-permute-start(f32[2,12,8,128]{3,2,1,0:T(8,128)S(1)} %get-tuple-element.33), channel_id=1, source_target_pairs={{0,16},{16,0},{32,48},{48,32},{64,80},{80,64},{96,112},{112,96},{1... | collective-permute-start | bytes 294920 | tf_op jit(solution)/shard_map/ppermute | solution.py:356
  52.1 2.0 %collective-permute-start.5 = (f32[2,12,8,128]{3,2,1,0:T(8,128)S(1)}, f32[2,12,8,128]{3,2,1,0:T(8,128)S(1)}, u32[]{:S(2)}, u32[]{:S(2)}) collective-permute-start(f32[2,12,8,128]{3,2,1,0:T(8,128)S(1)} %get-tuple-element.34), channel_id=1, source_target_pairs={{16,32},{32,16},{48,64},{64,48},{80,96},{96,80},{17,33},{33,17},{4... | collective-permute-start | bytes 294920 | tf_op jit(solution)/shard_map/ppermute | solution.py:356
  54.2 1.8 %collective-permute-done.4.refs_2_ = f32[2,12,8,128]{3,2,1,0:T(8,128)S(1)} collective-permute-done((f32[2,12,8,128]{3,2,1,0:T(8,128)S(1)}, f32[2,12,8,128]{3,2,1,0:T(8,128)S(1)}, u32[]{:S(2)}, u32[]{:S(2)}) %collective-permute-start.4) | collective-permute-done | bytes 98336 | tf_op jit(solution)/shard_map/ppermute | solution.py:356
  56.0 5.0 %collective-permute-done.5.refs_3_ = f32[2,12,8,128]{3,2,1,0:T(8,128)S(1)} collective-permute-done((f32[2,12,8,128]{3,2,1,0:T(8,128)S(1)}, f32[2,12,8,128]{3,2,1,0:T(8,128)S(1)}, u32[]{:S(2)}, u32[]{:S(2)}) %collective-permute-start.5) | collective-permute-done | bytes 98336 | tf_op jit(solution)/shard_map/ppermute | solution.py:356
  61.1 0.1 collective-permute-start.6
  61.2 5.2 %collective-permute-start.7 = (f32[4,12,8,128]{3,2,1,0:T(8,128)S(1)}, f32[4,12,8,128]{3,2,1,0:T(8,128)S(1)}, u32[]{:S(2)}, u32[]{:S(2)}) collective-permute-start(f32[4,12,8,128]{3,2,1,0:T(8,128)S(1)} %get-tuple-element.48), channel_id=1, source_target_pairs={{1,2},{2,1},{3,4},{4,3},{5,6},{6,5},{7,8},{8,7},{9,10},{10,9},{11,... | collective-permute-start | bytes 589832 | tf_op jit(solution)/shard_map/ppermute | solution.py:356
  66.4 3.9 %collective-permute-done.7.refs_5_ = f32[4,12,8,128]{3,2,1,0:T(8,128)S(1)} collective-permute-done((f32[4,12,8,128]{3,2,1,0:T(8,128)S(1)}, f32[4,12,8,128]{3,2,1,0:T(8,128)S(1)}, u32[]{:S(2)}, u32[]{:S(2)}) %collective-permute-start.7) | collective-permute-done | bytes 196640 | tf_op jit(solution)/shard_map/ppermute | solution.py:356
  70.3 26.8 %correct_pass.1 = (f32[4,12,8,128]{3,2,1,0:T(8,128)S(1)}, f32[7,192]{1,0:T(8,128)S(1)}, f32[7,192]{1,0:T(8,128)S(1)}) custom-call(f32[4,12,8,128]{3,2,1,0:T(8,128)S(1)} %fusion.6.refs_0_.refs_1_, f32[4,12,8,128]{3,2,1,0:T(8,128)S(1)} %get-tuple-element.32.refs_1_, f32[2,12,8,128]{3,2,1,0:T(8,128)S(1)} %collective-permute-done.4.refs_2_, ...), custom_call_target="tpu_custom_call" | custom-call | tf_op jit(solution)/shard_map/correct_pass/pallas_call | solution.py:377
  97.1 1.4 %collective-permute-start.8 = (f32[7,192]{1,0:T(8,128)S(1)}, f32[7,192]{1,0:T(8,128)S(1)}, u32[]{:S(2)}, u32[]{:S(2)}) collective-permute-start(f32[7,192]{1,0:T(8,128)S(1)} %get-tuple-element.36), channel_id=1, source_target_pairs={{0,16},{16,0},{32,48},{48,32},{64,80},{80,64},{96,112},{112,96},{1... | collective-permute-start | bytes 16136 | tf_op jit(solution)/shard_map/ppermute | solution.py:356
  98.5 1.9 %collective-permute-start.9 = (f32[7,192]{1,0:T(8,128)S(1)}, f32[7,192]{1,0:T(8,128)S(1)}, u32[]{:S(2)}, u32[]{:S(2)}) collective-permute-start(f32[7,192]{1,0:T(8,128)S(1)} %get-tuple-element.37), channel_id=1, source_target_pairs={{16,32},{32,16},{48,64},{64,48},{80,96},{96,80},{17,33},{33,17},{4... | collective-permute-start | bytes 16136 | tf_op jit(solution)/shard_map/ppermute | solution.py:356
  100.4 0.1 reshape.231
  100.5 0.8 broadcast_select_fusion
  101.3 1.1 collective-permute-done.8
  102.3 4.1 %collective-permute-done.9 = f32[7,192]{1,0:T(8,128)S(1)} collective-permute-done((f32[7,192]{1,0:T(8,128)S(1)}, f32[7,192]{1,0:T(8,128)S(1)}, u32[]{:S(2)}, u32[]{:S(2)}) %collective-permute-start.9) | collective-permute-done | bytes 5408 | tf_op jit(solution)/shard_map/ppermute | solution.py:356
  106.4 0.6 copy.17
  (32 shorter events, 0.5 us)
Async XLA Ops:
  1.4 0.9 copy-start
  2.9 9.0 %collective-permute-start.1 = (f32[2,12,8,128]{3,2,1,0:T(8,128)S(1)}, f32[2,12,8,128]{3,2,1,0:T(8,128)S(1)}, u32[]{:S(2)}, u32[]{:S(2)}) collective-permute-start(f32[2,12,8,128]{3,2,1,0:T(8,128)S(1)} %get-tuple-element.56), channel_id=1, source_target_pairs={{16,32},{32,16},{48,64},{64,48},{80,96},{96,80},{17,33},{33,17},{4... | collective-permute-start | bytes 294920 | tf_op jit(solution)/shard_map/ppermute | solution.py:356
  7.1 6.8 %collective-permute-start = (f32[2,12,8,128]{3,2,1,0:T(8,128)S(1)}, f32[2,12,8,128]{3,2,1,0:T(8,128)S(1)}, u32[]{:S(2)}, u32[]{:S(2)}) collective-permute-start(f32[2,12,8,128]{3,2,1,0:T(8,128)S(1)} %get-tuple-element.57), channel_id=1, source_target_pairs={{0,16},{16,0},{32,48},{48,32},{64,80},{80,64},{96,112},{112,96},{1... | collective-permute-start | bytes 294920 | tf_op jit(solution)/shard_map/ppermute | solution.py:356
  9.3 0.7 copy-start.1
  14.0 6.5 %collective-permute-start.2 = (f32[4,12,8,128]{3,2,1,0:T(8,128)S(1)}, f32[4,12,8,128]{3,2,1,0:T(8,128)S(1)}, u32[]{:S(2)}, u32[]{:S(2)}) collective-permute-start(f32[4,12,8,128]{3,2,1,0:T(8,128)S(1)} %get-tuple-element.51), channel_id=1, source_target_pairs={{0,1},{1,0},{2,3},{3,2},{4,5},{5,4},{6,7},{7,6},{8,9},{9,8},{10,11... | collective-permute-start | bytes 589832 | tf_op jit(solution)/shard_map/ppermute | solution.py:356
  14.1 9.5 %collective-permute-start.3 = (f32[4,12,8,128]{3,2,1,0:T(8,128)S(1)}, f32[4,12,8,128]{3,2,1,0:T(8,128)S(1)}, u32[]{:S(2)}, u32[]{:S(2)}) collective-permute-start(f32[4,12,8,128]{3,2,1,0:T(8,128)S(1)} %get-tuple-element.50), channel_id=1, source_target_pairs={{1,2},{2,1},{3,4},{4,3},{5,6},{6,5},{7,8},{8,7},{9,10},{10,9},{11,... | collective-permute-start | bytes 589832 | tf_op jit(solution)/shard_map/ppermute | solution.py:356
  49.8 6.2 %collective-permute-start.4 = (f32[2,12,8,128]{3,2,1,0:T(8,128)S(1)}, f32[2,12,8,128]{3,2,1,0:T(8,128)S(1)}, u32[]{:S(2)}, u32[]{:S(2)}) collective-permute-start(f32[2,12,8,128]{3,2,1,0:T(8,128)S(1)} %get-tuple-element.33), channel_id=1, source_target_pairs={{0,16},{16,0},{32,48},{48,32},{64,80},{80,64},{96,112},{112,96},{1... | collective-permute-start | bytes 294920 | tf_op jit(solution)/shard_map/ppermute | solution.py:356
  52.1 8.9 %collective-permute-start.5 = (f32[2,12,8,128]{3,2,1,0:T(8,128)S(1)}, f32[2,12,8,128]{3,2,1,0:T(8,128)S(1)}, u32[]{:S(2)}, u32[]{:S(2)}) collective-permute-start(f32[2,12,8,128]{3,2,1,0:T(8,128)S(1)} %get-tuple-element.34), channel_id=1, source_target_pairs={{16,32},{32,16},{48,64},{64,48},{80,96},{96,80},{17,33},{33,17},{4... | collective-permute-start | bytes 294920 | tf_op jit(solution)/shard_map/ppermute | solution.py:356
  61.1 5.3 %collective-permute-start.6 = (f32[4,12,8,128]{3,2,1,0:T(8,128)S(1)}, f32[4,12,8,128]{3,2,1,0:T(8,128)S(1)}, u32[]{:S(2)}, u32[]{:S(2)}) collective-permute-start(f32[4,12,8,128]{3,2,1,0:T(8,128)S(1)} %get-tuple-element.49), channel_id=1, source_target_pairs={{0,1},{1,0},{2,3},{3,2},{4,5},{5,4},{6,7},{7,6},{8,9},{9,8},{10,11... | collective-permute-start | bytes 589832 | tf_op jit(solution)/shard_map/ppermute | solution.py:356
  61.2 9.1 %collective-permute-start.7 = (f32[4,12,8,128]{3,2,1,0:T(8,128)S(1)}, f32[4,12,8,128]{3,2,1,0:T(8,128)S(1)}, u32[]{:S(2)}, u32[]{:S(2)}) collective-permute-start(f32[4,12,8,128]{3,2,1,0:T(8,128)S(1)} %get-tuple-element.48), channel_id=1, source_target_pairs={{1,2},{2,1},{3,4},{4,3},{5,6},{6,5},{7,8},{8,7},{9,10},{10,9},{11,... | collective-permute-start | bytes 589832 | tf_op jit(solution)/shard_map/ppermute | solution.py:356
  97.1 5.2 %collective-permute-start.8 = (f32[7,192]{1,0:T(8,128)S(1)}, f32[7,192]{1,0:T(8,128)S(1)}, u32[]{:S(2)}, u32[]{:S(2)}) collective-permute-start(f32[7,192]{1,0:T(8,128)S(1)} %get-tuple-element.36), channel_id=1, source_target_pairs={{0,16},{16,0},{32,48},{48,32},{64,80},{80,64},{96,112},{112,96},{1... | collective-permute-start | bytes 16136 | tf_op jit(solution)/shard_map/ppermute | solution.py:356
  98.5 7.9 %collective-permute-start.9 = (f32[7,192]{1,0:T(8,128)S(1)}, f32[7,192]{1,0:T(8,128)S(1)}, u32[]{:S(2)}, u32[]{:S(2)}) collective-permute-start(f32[7,192]{1,0:T(8,128)S(1)} %get-tuple-element.37), channel_id=1, source_target_pairs={{16,32},{32,16},{48,64},{64,48},{80,96},{96,80},{17,33},{33,17},{4... | collective-permute-start | bytes 16136 | tf_op jit(solution)/shard_map/ppermute | solution.py:356
